TPU v7x, 32 devices: a whole 2x2x4 slice. The times are simulated.
32 devices in a mesh: fsdp: 32 (over z, y, x, core).
Axes of the slice: x: 2, y: 2, z: 4, core: 2. Of those that a mesh axis runs over, the one named last changes fastest.
Arguments:
- tokens: bfloat16 [32, 512, 1024], P('fsdp'), may hold values from -6 to 6
- cotangent: bfloat16 [32, 512, 1024], P('fsdp'), may hold values from -6 to 6
- segments: int32 [32, 512], P('fsdp'), may hold values from 0 to 25, as said below
- adapter_id: int32 [32], P('fsdp'), may hold values from 0 to 7
- input_weight: bfloat16 [3, 1024, 1024], P(None, 'fsdp'), may hold values from -0.1875 to 0.1875
- output_weight: bfloat16 [1024, 1024], P('fsdp'), may hold values from -0.75 to 0.75
- norm_gain: bfloat16 [2, 1024], P(None, 'fsdp'), may hold values from 0.5 to 1.5
- norm_shift: bfloat16 [2, 1024], P(None, 'fsdp'), may hold values from -1.75 to 1.75
- attention_down: bfloat16 [4, 8, 1024, 16], P(None, None, 'fsdp'), may hold values from -0.1875 to 0.1875
- attention_up: bfloat16 [4, 8, 16, 1024], P(None, None, None, 'fsdp'), may hold values from -0.75 to 0.75
- expand_weight: bfloat16 [1024, 4096], P('fsdp'), may hold values from -0.1875 to 0.1875
- reduce_weight: bfloat16 [4096, 1024], P('fsdp'), may hold values from -0.09375 to 0.09375
- expand_down: bfloat16 [8, 1024, 16], P(None, 'fsdp'), may hold values from -0.1875 to 0.1875
- expand_up: bfloat16 [8, 16, 4096], P(None, None, 'fsdp'), may hold values from -0.75 to 0.75
- reduce_down: bfloat16 [8, 4096, 16], P(None, 'fsdp'), may hold values from -0.09375 to 0.09375
- reduce_up: bfloat16 [8, 16, 1024], P(None, None, 'fsdp'), may hold values from -0.75 to 0.75
Outputs:
- layer_output: bfloat16 [32, 512, 1024], P('fsdp')
- input_gradient: float32 [32, 512, 1024], P('fsdp')
- attention_down_gradient: float32 [4, 8, 1024, 16], P(None, None, 'fsdp')
- attention_up_gradient: float32 [4, 8, 16, 1024], P(None, None, None, 'fsdp')
- expand_down_gradient: float32 [8, 1024, 16], P(None, 'fsdp')
- expand_up_gradient: float32 [8, 16, 4096], P(None, None, 'fsdp')
- reduce_down_gradient: float32 [8, 4096, 16], P(None, 'fsdp')
- reduce_up_gradient: float32 [8, 16, 1024], P(None, None, 'fsdp')
Inputs may be any that keep to these rules, and one draw needn't show every extreme that they name: `segments`: in each sequence the numbers start at 0 at the first token and rise by one at each document's first token; every document but a sequence's last has 20 to 200 tokens; in one sequence of every draw every document but the last has exactly 20 tokens.
All inputs are finite; a program needn't handle non-finite values.
Results may differ from a plain program's by a relative error of at most 0.015.
Values may be sent and summed in bfloat16 or wider, within the bound.
No kernel may reach another device: no remote copies, remote signals or barrier semaphores. Data moves between devices by JAX's collectives and lax.ppermute only.
A program may use at most 192 MiB of HBM per device.

v0:
```python
import jax
import jax.numpy as jnp
from jax import lax
from jax.sharding import PartitionSpec as P

HEAD_DIM = 64


epsilon = 1e-12


def layer_norm(values, gains, shifts):
    average = jnp.mean(values, axis=-1, keepdims=True)
    centered = values - average
    spread = jnp.mean(centered * centered, axis=-1, keepdims=True)
    return centered * lax.rsqrt(spread + epsilon) * gains + shifts


def exact_gelu(values):
    return jax.nn.gelu(values, approximate=False)


def product(form, left, right):
    return jnp.einsum(form, left, right, preferred_element_type=jnp.float32)


def prepare_attention(gathered, chosen):
    picked_down = product("sa,paxr->psxr", chosen, gathered[2]).astype(jnp.bfloat16)
    picked_up = product("sa,pare->psre", chosen, gathered[3]).astype(jnp.bfloat16)
    return (gathered[0], gathered[1], picked_down, picked_up)


def prepare_feed(gathered, chosen):
    expand_picked_down = product("sa,axr->sxr", chosen, gathered[2]).astype(jnp.bfloat16)
    expand_picked_up = product("sa,are->sre", chosen, gathered[3]).astype(jnp.bfloat16)
    reduce_picked_down = product("sa,axr->sxr", chosen, gathered[4]).astype(jnp.bfloat16)
    reduce_picked_up = product("sa,are->sre", chosen, gathered[5]).astype(jnp.bfloat16)
    return (
        gathered[0],
        gathered[1],
        expand_picked_down,
        expand_picked_up,
        reduce_picked_down,
        reduce_picked_up,
    )


def per_adapter(chosen_wide, terms):
    return jnp.sum(chosen_wide[:, :, None, None] * terms[:, None], axis=0)


def per_adapter_stacked(chosen_wide, terms):
    return jnp.sum(chosen_wide.T[None, :, :, None, None] * terms[:, None], axis=2)


def masked_scores(queries, key_rows, segment):
    scores = product("qhd,khd->hqk", queries, key_rows) * HEAD_DIM ** (-0.5)
    same_doc = segment[:, None] == segment[None, :]
    return jnp.where(same_doc[None], scores, -1000000000.0)


def attend_forward(parts):
    queries, key_rows, value_rows, segment = parts
    length = queries.shape[0]
    head_count = queries.shape[1] // HEAD_DIM
    shaped_query = queries.reshape(length, head_count, HEAD_DIM)
    shaped_keys = key_rows.reshape(length, head_count, HEAD_DIM)
    shaped_values = value_rows.reshape(length, head_count, HEAD_DIM)
    masked = masked_scores(shaped_query, shaped_keys, segment)
    largest = jnp.max(masked, axis=-1, keepdims=True)
    log_total = largest + jnp.log(jnp.sum(jnp.exp(masked - largest), axis=-1, keepdims=True))
    weights = jnp.exp(masked - log_total).astype(jnp.bfloat16)
    context = product("hqk,khd->qhd", weights, shaped_values).reshape(length, head_count * HEAD_DIM)
    return (context.astype(jnp.bfloat16), log_total)


def attend_backward(parts):
    queries, key_rows, value_rows, segment, log_total, context_back = parts
    length = queries.shape[0]
    head_count = queries.shape[1] // HEAD_DIM
    scaling = HEAD_DIM ** (-0.5)
    shaped_query = queries.reshape(length, head_count, HEAD_DIM)
    shaped_keys = key_rows.reshape(length, head_count, HEAD_DIM)
    shaped_values = value_rows.reshape(length, head_count, HEAD_DIM)
    shaped_back = context_back.reshape(length, head_count, HEAD_DIM)
    masked = masked_scores(shaped_query, shaped_keys, segment)
    weights = jnp.exp(masked - log_total)
    weights_back = product("qhd,khd->hqk", shaped_back, shaped_values)
    row_dots = jnp.sum(weights * weights_back, axis=-1, keepdims=True)
    scores_back = (weights * (weights_back - row_dots)).astype(jnp.bfloat16)
    query_back = (product("hqk,khd->qhd", scores_back, shaped_keys) * scaling).reshape(length, -1)
    key_back = (product("hqk,qhd->khd", scores_back, shaped_query) * scaling).reshape(length, -1)
    value_back = product("hqk,qhd->khd", weights.astype(jnp.bfloat16), shaped_back).reshape(
        length, -1
    )
    return (
        query_back.astype(jnp.bfloat16),
        key_back.astype(jnp.bfloat16),
        value_back.astype(jnp.bfloat16),
    )


def on_device(
    tokens,
    cotangent,
    segments,
    adapter_id,
    input_weight,
    output_weight,
    norm_gain,
    norm_shift,
    attention_down,
    attention_up,
    expand_weight,
    reduce_weight,
    expand_down,
    expand_up,
    reduce_down,
    reduce_up,
):
    adapter_count = attention_down.shape[1]
    chosen = (adapter_id[:, None] == jnp.arange(adapter_count, dtype=jnp.int32)[None, :]).astype(
        jnp.bfloat16
    )
    chosen_wide = chosen.astype(jnp.float32)
    attention_whole = (
        lax.all_gather(input_weight, "fsdp", axis=1, tiled=True),
        lax.all_gather(output_weight, "fsdp", axis=0, tiled=True),
        lax.all_gather(attention_down, "fsdp", axis=2, tiled=True),
        lax.all_gather(attention_up, "fsdp", axis=3, tiled=True),
        lax.all_gather(norm_gain, "fsdp", axis=1, tiled=True),
        lax.all_gather(norm_shift, "fsdp", axis=1, tiled=True),
    )
    attention_tables = prepare_attention(attention_whole, chosen)
    gain_whole = attention_whole[4].astype(jnp.float32)
    shift_whole = attention_whole[5].astype(jnp.float32)
    inner_qkv = product("slx,psxr->pslr", tokens, attention_tables[2][:3]).astype(jnp.bfloat16)
    projected = (
        product("slx,pxe->psle", tokens, attention_tables[0])
        + product("pslr,psre->psle", inner_qkv, attention_tables[3][:3])
    ).astype(jnp.bfloat16)
    context, log_total = lax.map(
        attend_forward, (projected[0], projected[1], projected[2], segments)
    )
    feed_whole = (
        lax.all_gather(expand_weight, "fsdp", axis=0, tiled=True),
        lax.all_gather(reduce_weight, "fsdp", axis=0, tiled=True),
        lax.all_gather(expand_down, "fsdp", axis=1, tiled=True),
        lax.all_gather(expand_up, "fsdp", axis=2, tiled=True),
        lax.all_gather(reduce_down, "fsdp", axis=1, tiled=True),
        lax.all_gather(reduce_up, "fsdp", axis=2, tiled=True),
    )
    inner_out = product("slx,sxr->slr", context, attention_tables[2][3]).astype(jnp.bfloat16)
    branch = product("slx,xe->sle", context, attention_tables[1]) + product(
        "slr,sre->sle", inner_out, attention_tables[3][3]
    )
    hidden_one = tokens.astype(jnp.float32) + branch
    normed, norm_one_back = jax.vjp(
        lambda values: layer_norm(values, gain_whole[0], shift_whole[0]), hidden_one
    )
    normed_low = normed.astype(jnp.bfloat16)
    feed_tables = prepare_feed(feed_whole, chosen)
    inner_expand = product("slx,sxr->slr", normed_low, feed_tables[2]).astype(jnp.bfloat16)
    expanded = product("slx,xf->slf", normed_low, feed_tables[0]) + product(
        "slr,srf->slf", inner_expand, feed_tables[3]
    )
    active, gelu_back = jax.vjp(exact_gelu, expanded)
    active_low = active.astype(jnp.bfloat16)
    inner_reduce = product("slf,sfr->slr", active_low, feed_tables[4]).astype(jnp.bfloat16)
    reduced = product("slf,fe->sle", active_low, feed_tables[1]) + product(
        "slr,sre->sle", inner_reduce, feed_tables[5]
    )
    hidden_two = normed + reduced
    output, norm_two_back = jax.vjp(
        lambda values: layer_norm(values, gain_whole[1], shift_whole[1]), hidden_two
    )
    feed_later = prepare_feed(
        (
            lax.all_gather(expand_weight, "fsdp", axis=0, tiled=True),
            lax.all_gather(reduce_weight, "fsdp", axis=0, tiled=True),
            lax.all_gather(expand_down, "fsdp", axis=1, tiled=True),
            lax.all_gather(expand_up, "fsdp", axis=2, tiled=True),
            lax.all_gather(reduce_down, "fsdp", axis=1, tiled=True),
            lax.all_gather(reduce_up, "fsdp", axis=2, tiled=True),
        ),
        chosen,
    )
    two_back = norm_two_back(cotangent.astype(jnp.float32))[0]
    reduced_back = two_back.astype(jnp.bfloat16)
    inner_reduce_back = product("sle,sre->slr", reduced_back, feed_later[5]).astype(jnp.bfloat16)
    active_back = product("sle,fe->slf", reduced_back, feed_later[1]) + product(
        "slr,sfr->slf", inner_reduce_back, feed_later[4]
    )
    expanded_back = gelu_back(active_back)[0].astype(jnp.bfloat16)
    inner_expand_back = product("slf,srf->slr", expanded_back, feed_later[3]).astype(jnp.bfloat16)
    normed_back = (
        two_back
        + product("slf,xf->slx", expanded_back, feed_later[0])
        + product("slr,sxr->slx", inner_expand_back, feed_later[2])
    )
    feed_terms = (
        per_adapter(chosen_wide, product("slx,slr->sxr", normed_low, inner_expand_back)),
        per_adapter(chosen_wide, product("slr,slf->srf", inner_expand, expanded_back)),
        per_adapter(chosen_wide, product("slf,slr->sfr", active_low, inner_reduce_back)),
        per_adapter(chosen_wide, product("slr,sle->sre", inner_reduce, reduced_back)),
    )
    feed_grads = (
        lax.psum_scatter(feed_terms[0], "fsdp", scatter_dimension=1, tiled=True),
        lax.psum_scatter(feed_terms[1], "fsdp", scatter_dimension=2, tiled=True),
        lax.psum_scatter(feed_terms[2], "fsdp", scatter_dimension=1, tiled=True),
        lax.psum_scatter(feed_terms[3], "fsdp", scatter_dimension=2, tiled=True),
    )
    one_back = norm_one_back(normed_back)[0]
    branch_back = one_back.astype(jnp.bfloat16)
    attention_later = prepare_attention(
        (
            lax.all_gather(input_weight, "fsdp", axis=1, tiled=True),
            lax.all_gather(output_weight, "fsdp", axis=0, tiled=True),
            lax.all_gather(attention_down, "fsdp", axis=2, tiled=True),
            lax.all_gather(attention_up, "fsdp", axis=3, tiled=True),
        ),
        chosen,
    )
    inner_out_back = product("sle,sre->slr", branch_back, attention_later[3][3]).astype(
        jnp.bfloat16
    )
    context_back = (
        product("sle,xe->slx", branch_back, attention_later[1])
        + product("slr,sxr->slx", inner_out_back, attention_later[2][3])
    ).astype(jnp.bfloat16)
    query_back, key_back, value_back = lax.map(
        attend_backward,
        (projected[0], projected[1], projected[2], segments, log_total, context_back),
    )
    projected_back = jnp.stack([query_back, key_back, value_back])
    inner_qkv_back = product("psle,psre->pslr", projected_back, attention_later[3][:3]).astype(
        jnp.bfloat16
    )
    tokens_back = (
        one_back
        + product("psle,pxe->slx", projected_back, attention_later[0])
        + product("pslr,psxr->slx", inner_qkv_back, attention_later[2][:3])
    )
    up_terms = jnp.concatenate(
        [
            product("pslr,psle->psre", inner_qkv, projected_back),
            product("slr,sle->sre", inner_out, branch_back)[None],
        ],
        axis=0,
    )
    down_terms = jnp.concatenate(
        [
            product("slx,pslr->psxr", tokens, inner_qkv_back),
            product("slx,slr->sxr", context, inner_out_back)[None],
        ],
        axis=0,
    )
    attention_grads = (
        lax.psum_scatter(
            per_adapter_stacked(chosen_wide, down_terms), "fsdp", scatter_dimension=2, tiled=True
        ),
        lax.psum_scatter(
            per_adapter_stacked(chosen_wide, up_terms), "fsdp", scatter_dimension=3, tiled=True
        ),
    )
    return (
        output.astype(jnp.bfloat16),
        tokens_back,
        attention_grads[0],
        attention_grads[1],
        feed_grads[0],
        feed_grads[1],
        feed_grads[2],
        feed_grads[3],
    )


def solution(mesh):
    placed = (
        P("fsdp", None, None),
        P("fsdp", None, None),
        P("fsdp", None),
        P("fsdp"),
        P(None, "fsdp", None),
        P("fsdp", None),
        P(None, "fsdp"),
        P(None, "fsdp"),
        P(None, None, "fsdp", None),
        P(None, None, None, "fsdp"),
        P("fsdp", None),
        P("fsdp", None),
        P(None, "fsdp", None),
        P(None, None, "fsdp"),
        P(None, "fsdp", None),
        P(None, None, "fsdp"),
    )
    return jax.shard_map(
        on_device,
        mesh=mesh,
        in_specs=placed,
        out_specs=(
            P("fsdp", None, None),
            P("fsdp", None, None),
            P(None, None, "fsdp", None),
            P(None, None, None, "fsdp"),
            P(None, "fsdp", None),
            P(None, None, "fsdp"),
            P(None, "fsdp", None),
            P(None, None, "fsdp"),
        ),
        check_vma=False,
    )
```

profile of v0, /device:TPU:0, one launch (start us, length us, event | category | flops | bytes accessed | tf_op | source)
XLA Modules:
  0.0 1451.6 jit_solution(18230189441551955992)
XLA Ops:
  7.2 2.0 copy.75
  9.3 2.0 copy.76
  16.5 43.7 %all-gather = bf16[32,32,2]{1,2,0:T(2,128)(2,1)S(1)} all-gather(bf16[1,32,2]{1,2,0:T(2,128)(2,1)} %bitcast.271), channel_id=1, replica_groups=mesh['fsdp'=32] {'fsdp'}, dimensions={0}, use_global_device_ids=true | all-gather | bytes 4224 | tf_op jit(solution)/shard_map/all_gather | solution.py:131
  60.9 37.9 %all-gather.1 = bf16[32,32,2]{1,2,0:T(2,128)(2,1)S(1)} all-gather(bf16[1,32,2]{1,2,0:T(2,128)(2,1)} %bitcast.272), channel_id=1, replica_groups=mesh['fsdp'=32] {'fsdp'}, dimensions={0}, use_global_device_ids=true | all-gather | bytes 4224 | tf_op jit(solution)/shard_map/all_gather | solution.py:132
  102.2 47.0 %all_gather.57 = bf16[8,16,1024]{1,0,2:T(8,128)(2,1)S(1)} all-gather(bf16[8,16,32]{1,0,2:T(8,128)(2,1)S(1)} %copy.82), channel_id=1, replica_groups=mesh['fsdp'=32] {'fsdp'}, dimensions={2}, use_global_device_ids=true | all-gather | bytes 270336 | tf_op jit(solution)/shard_map/all_gather | solution.py:151
  149.3 1.7 copy.105
  150.9 53.9 %all_gather.53 = bf16[8,1024,16]{2,0,1:T(8,128)(2,1)S(1)} all-gather(bf16[8,32,16]{2,0,1:T(8,128)(2,1)S(1)} %copy.81), channel_id=1, replica_groups=mesh['fsdp'=32] {'fsdp'}, dimensions={1}, use_global_device_ids=true | all-gather | bytes 270336 | tf_op jit(solution)/shard_map/all_gather | solution.py:148
  205.7 2.2 multiply_reduce_fusion.1
  207.9 9.3 copy.91
  217.7 9.1 copy.94
  227.4 9.4 all-gather.25.cloned.1.call-done
  236.8 11.0 fusion.19
  247.8 14.0 copy.104
  262.2 25.4 %all-gather.21.cloned.1.call-done = bf16[8,16,4096]{2,1,0:T(8,128)(2,1)} async-done(((bf16[8,16,128]{2,1,0:T(8,128)(2,1)}), bf16[8,16,4096]{2,1,0:T(8,128)(2,1)}) %all-gather.21.cloned.1.call-update) | async-done | bytes 1048592 | tf_op jit(solution)/shard_map/all_gather | solution.py:149
  287.6 3.2 fusion.21
  290.9 68.4 %all-gather.11.cloned.1.call-done = bf16[3,1024,1024]{2,1,0:T(8,128)(2,1)} async-done(((bf16[3,32,1024]{2,1,0:T(8,128)(2,1)}), bf16[3,1024,1024]{2,1,0:T(8,128)(2,1)}) %all-gather.11.cloned.1.call-update) | async-done | bytes 6291472 | tf_op jit(solution)/shard_map/all_gather | solution.py:127
  359.2 5.6 fusion.17
  366.1 7.6 fusion
  373.8 9.2 exponential_reduce_fusion
  383.0 8.2 convolution_convert_fusion.1
  391.4 25.4 %all-gather.17.cloned.1.call-done = bf16[1024,1024]{1,0:T(8,128)(2,1)} async-done(((bf16[32,1024]{1,0:T(8,128)(2,1)}), bf16[1024,1024]{1,0:T(8,128)(2,1)}) %all-gather.17.cloned.1.call-update) | async-done | bytes 2097168 | tf_op jit(solution)/shard_map/all_gather | solution.py:128
  416.8 2.9 fusion.59
  419.7 1.3 fusion.57
  422.8 72.8 %all-gather.19.cloned.1.call-done = bf16[1024,4096]{1,0:T(8,128)(2,1)} async-done(((bf16[32,4096]{1,0:T(8,128)(2,1)}), bf16[1024,4096]{1,0:T(8,128)(2,1)}) %all-gather.19.cloned.1.call-update) | async-done | bytes 8388624 | tf_op jit(solution)/shard_map/all_gather | solution.py:146
  495.6 6.9 fusion.60
  502.5 21.3 %multiply_convert_fusion.1 = (bf16[512,4096]{1,0:T(8,128)(2,1)S(1)}, f32[512,4096]{1,0:T(8,128)}, f32[512,4096]{1,0:T(8,128)}) fusion(f32[512,4096]{1,0:T(8,128)S(1)} %fusion.60, bf16[512,16]{0,1:T(8,128)(2,1)S(1)} %convolution_convert_fusion.7, bf16[1,16,4096]{2,0,1:T(2,128)(2,1)S(1)} %copy-done.26), kind=kOutput, calls=%fused_computation.10 | convolution fusion | flops 205520896 | bytes 29507584 | tf_op jit(solution)/shard_map/slr,srf->slf/dot_general | solution.py:24
  523.8 2.0 copy-done.3
  527.0 47.1 %all-gather.23.cloned.1.call-done = bf16[4096,1024]{1,0:T(8,128)(2,1)} async-done(((bf16[128,1024]{1,0:T(8,128)(2,1)}), bf16[4096,1024]{1,0:T(8,128)(2,1)}) %all-gather.23.cloned.1.call-update) | async-done | bytes 8388624 | tf_op jit(solution)/shard_map/all_gather | solution.py:147
  574.1 8.2 fusion.61
  584.3 1.9 fusion.52
  587.0 10.3 fusion.62
  597.3 10.6 add_convert_fusion
  609.4 4.5 fusion.63
  619.0 1.3 fusion.64
  621.3 3.6 copy.116
  624.9 4.0 reshape.619
  629.0 3.8 copy.114
  632.8 3.9 reshape.617
  636.7 11.8 multiply_reduce_fusion
  648.5 12.3 multiply_convert_fusion
  660.9 3.3 copy-done
  664.2 3.6 multiply_convert_fusion.2
  667.8 9.1 convolution_convert_fusion
  676.9 4.8 multiply_convert_fusion.3
  681.8 1.7 copy.89
  683.6 1.3 copy.87
  684.9 1.5 copy.88
  687.4 1.8 convolution_bitcast_fusion
  689.5 13.6 copy.112
  703.1 15.1 %reshape.615 = f32[1024,512]{1,0:T(8,128)} reshape(f32[1024,4,8,16]{3,2,1,0:T(8,128)} %bitcast.230) | data formatting | bytes 4194304
  718.6 2.5 convolution_convert_fusion.3
  722.4 13.6 copy.110
  735.9 14.9 %reshape.613 = f32[1024,512]{1,0:T(8,128)} reshape(f32[1024,4,8,16]{3,2,1,0:T(8,128)} %bitcast.231) | data formatting | bytes 4194304
  751.0 2.8 fusion.65
  753.8 1.6 broadcast_multiply_fusion.1
  755.8 2.9 fusion.68
  758.7 1.6 broadcast_multiply_fusion
  760.4 6.4 fusion.50
  766.8 1.8 bitcast_add_fusion.1
  770.1 127.2 %reduce-scatter.23.cloned.1.call-done = f32[32,128]{1,0:T(8,128)} async-done(((f32[1024,128]{1,0:T(8,128)}), f32[32,128]{1,0:T(8,128)}) %reduce-scatter.23.cloned.1.call-update) | async-done | bytes 16400
  898.9 135.0 %reduce-scatter.21.cloned.1.call-done = f32[32,512]{1,0:T(8,128)} async-done(((f32[1024,512]{1,0:T(8,128)}), f32[32,512]{1,0:T(8,128)}) %reduce-scatter.21.cloned.1.call-update) | async-done | bytes 65552
  1036.0 134.4 %reduce-scatter.19.cloned.1.call-done = f32[32,512]{1,0:T(8,128)} async-done(((f32[1024,512]{1,0:T(8,128)}), f32[32,512]{1,0:T(8,128)}) %reduce-scatter.19.cloned.1.call-update) | async-done | bytes 65552
  1172.4 135.1 %reduce-scatter.15.cloned.1.call-done = f32[8,16,128]{2,1,0:T(8,128)} async-done(((f32[8,16,4096]{2,1,0:T(8,128)}), f32[8,16,128]{2,1,0:T(8,128)}) %reduce-scatter.15.cloned.1.call-update) | async-done | bytes 65552 | tf_op jit(solution)/shard_map/reduce_scatter | solution.py:209
  1307.5 137.1 %reduce-scatter.17.cloned.1.call-done = f32[8,128,16]{1,2,0:T(8,128)} async-done(((f32[8,4096,16]{1,2,0:T(8,128)}), f32[8,128,16]{1,2,0:T(8,128)}) %reduce-scatter.17.cloned.1.call-update) | async-done | bytes 65552 | tf_op jit(solution)/shard_map/reduce_scatter | solution.py:210
  (218 shorter events, 36.3 us)
Async XLA Ops:
  7.2 200.8 %all-gather.13.cloned.1.call-start = ((), (), s32[]{:S(2)}) async-start(), calls=%async_computation.7 | async-start | bytes 8650752 | tf_op jit(solution)/shard_map/all_gather | solution.py:129
  9.2 208.5 %all-gather.15.cloned.1.call-start = ((), (), s32[]{:S(2)}) async-start(), calls=%async_computation.8 | async-start | bytes 8650752 | tf_op jit(solution)/shard_map/all_gather | solution.py:130
  11.3 225.5 %all-gather.25.cloned.1.call-start = ((), (), s32[]{:S(2)}) async-start(), calls=%async_computation.13 | async-start | bytes 1081344 | tf_op jit(solution)/shard_map/all_gather | solution.py:150
  12.1 275.6 %all-gather.21.cloned.1.call-start = ((), (), s32[]{:S(2)}) async-start(), calls=%async_computation.11 | async-start | bytes 1081344 | tf_op jit(solution)/shard_map/all_gather | solution.py:149
  12.6 346.6 %all-gather.11.cloned.1.call-start = ((), (), s32[]{:S(2)}) async-start(), calls=%async_computation.6 | async-start | bytes 6488064 | tf_op jit(solution)/shard_map/all_gather | solution.py:127
  13.2 403.5 %all-gather.17.cloned.1.call-start = ((), (), s32[]{:S(2)}) async-start(), calls=%async_computation.9 | async-start | bytes 2162688 | tf_op jit(solution)/shard_map/all_gather | solution.py:128
  13.8 481.8 %all-gather.19.cloned.1.call-start = ((), (), s32[]{:S(2)}) async-start(), calls=%async_computation.10 | async-start | bytes 8650752 | tf_op jit(solution)/shard_map/all_gather | solution.py:146
  14.6 559.6 %all-gather.23.cloned.1.call-start = ((), (), s32[]{:S(2)}) async-start(), calls=%async_computation.12 | async-start | bytes 8650752 | tf_op jit(solution)/shard_map/all_gather | solution.py:147
  15.3 753.3 %reduce-scatter.25.cloned.1.call-start = ((), (), s32[]{:S(2)}) async-start(), calls=%async_computation.19 | async-start | bytes 540672
  227.4 137.5 %copy-start.24 = (bf16[1,4,16,1024]{3,2,1,0:T(8,128)(2,1)}, bf16[1,4,16,1024]{3,2,1,0:T(8,128)(2,1)S(1)}, u32[]{:S(2)}) copy-start(bf16[1,4,16,1024]{3,2,1,0:T(8,128)(2,1)S(1)} %copy.136) | copy-start | bytes 393220
  247.8 14.0 copy-start.7
  262.2 102.6 %copy-start.33 = (bf16[3,512,16]{1,2,0:T(8,128)(2,1)}, bf16[3,512,16]{1,2,0:T(8,128)(2,1)S(1)}, u32[]{:S(2)}) copy-start(bf16[3,512,16]{1,2,0:T(8,128)(2,1)S(1)} %fusion.11) | copy-start | bytes 147460
  366.1 7.6 copy-start.5
  366.1 7.6 copy-start.11
  366.1 16.8 %copy-start.13 = (bf16[1,1,512,1024]{2,3,0,1:T(8,128)(2,1)}, bf16[1,1,512,1024]{2,3,0,1:T(8,128)(2,1)S(1)}, u32[]{:S(2)}) copy-start(bf16[1,1,512,1024]{2,3,0,1:T(8,128)(2,1)S(1)} %get-tuple-element.69) | copy-start | bytes 3145732
  383.0 8.2 copy-start.30
  391.2 25.6 %copy-start.9 = (bf16[16,64,512]{2,1,0:T(8,128)(2,1)}, bf16[16,64,512]{2,1,0:T(8,128)(2,1)S(1)}, u32[]{:S(2)}) copy-start(bf16[16,64,512]{2,1,0:T(8,128)(2,1)S(1)} %convolution_convert_fusion.1) | copy-start | bytes 3145732
  391.4 30.0 %copy-start.37 = (bf16[512,16]{0,1:T(8,128)(2,1)}, bf16[512,16]{0,1:T(8,128)(2,1)S(1)}, u32[]{:S(2)}) copy-start(bf16[512,16]{0,1:T(8,128)(2,1)S(1)} %convolution_convert_fusion.4) | copy-start | bytes 49156
  416.8 5.2 copy-start.43
  416.8 5.2 copy-start.48
  422.8 79.8 %copy-start.45 = (bf16[512,16]{0,1:T(8,128)(2,1)}, bf16[512,16]{0,1:T(8,128)(2,1)S(1)}, u32[]{:S(2)}) copy-start(bf16[512,16]{0,1:T(8,128)(2,1)S(1)} %convolution_convert_fusion.7) | copy-start | bytes 49156
  495.6 7.0 copy-start.26
  502.5 23.3 %copy-start.28 = (bf16[1,4096,16]{1,2,0:T(8,128)(2,1)S(1)}, bf16[1,4096,16]{1,2,0:T(8,128)(2,1)}, u32[]{:S(2)}) copy-start(bf16[1,4096,16]{1,2,0:T(8,128)(2,1)} %copy.104) | copy-start | bytes 393220
  574.1 8.2 copy-start.32
  574.1 8.2 copy-start.40
  574.1 8.2 copy-start.44
  574.1 8.2 copy-start.49
  574.1 8.2 copy-start.51
  586.7 10.6 copy-start.41
  587.0 10.3 copy-start.29
  587.0 22.4 %slice-start = ((s8[8388608]{0:T(1024)(128)(4,1)}), s8[4194304]{0:T(1024)(128)(4,1)S(1)}, s32[]{:S(2)}) async-start(s8[8388608]{0:T(1024)(128)(4,1)} %bitcast.273), calls=%async_computation.20 | async-start | bytes 8388608
  597.3 10.6 copy-start.27
  597.3 12.1 slice-start.1
  607.9 6.0 copy-start.4
  609.4 4.6 copy-start.17
  614.9 4.0 copy-start.18
  615.6 4.7 copy-start.1
  615.7 4.7 copy-start.56
  624.9 11.8 copy-start.14
  628.9 268.4 %reduce-scatter.23.cloned.1.call-start = ((), (), s32[]{:S(2)}) async-start(), calls=%async_computation.18 | async-start | bytes 540672
  636.7 11.8 copy-start.31
  648.5 15.6 %copy-start.12 = (bf16[1,1,512,1024]{2,3,0,1:T(8,128)(2,1)S(1)}, bf16[1,1,512,1024]{2,3,0,1:T(8,128)(2,1)}, u32[]{:S(2)}) copy-start(bf16[1,1,512,1024]{2,3,0,1:T(8,128)(2,1)} %copy-done.11) | copy-start | bytes 3145732
  660.9 3.3 copy-start
  667.8 9.1 copy-start.6
  676.9 357.1 %reduce-scatter.21.cloned.1.call-start = ((), (), s32[]{:S(2)}) async-start(), calls=%async_computation.17 | async-start | bytes 2162688
  681.8 4.6 copy-start.38
  681.8 5.6 copy-start.34
  683.5 5.6 copy-start.19
  683.5 5.6 copy-start.53
  703.1 15.2 %copy-start.10 = (bf16[16,64,512]{2,1,0:T(8,128)(2,1)S(1)}, bf16[16,64,512]{2,1,0:T(8,128)(2,1)}, u32[]{:S(2)}) copy-start(bf16[16,64,512]{2,1,0:T(8,128)(2,1)} %copy-done.9) | copy-start | bytes 3145732
  703.1 15.6 %copy-start.20 = (bf16[1,1,512,1024]{3,2,0,1:T(8,128)(2,1)S(1)}, bf16[1,1,512,1024]{3,2,0,1:T(8,128)(2,1)}, u32[]{:S(2)}) copy-start(bf16[1,1,512,1024]{3,2,0,1:T(8,128)(2,1)} %copy-done.19) | copy-start | bytes 3145732
  703.1 15.6 %copy-start.25 = (bf16[1,4,16,1024]{3,2,1,0:T(8,128)(2,1)S(1)}, bf16[1,4,16,1024]{3,2,1,0:T(8,128)(2,1)}, u32[]{:S(2)}) copy-start(bf16[1,4,16,1024]{3,2,1,0:T(8,128)(2,1)} %copy-done.24) | copy-start | bytes 393220
  718.1 3.6 copy-start.8
  718.2 452.2 %reduce-scatter.19.cloned.1.call-start = ((), (), s32[]{:S(2)}) async-start(), calls=%async_computation.16 | async-start | bytes 2162688
  718.2 3.8 copy-start.54
  735.9 15.0 %copy-start.46 = (bf16[512,16]{0,1:T(8,128)(2,1)S(1)}, bf16[512,16]{0,1:T(8,128)(2,1)}, u32[]{:S(2)}) copy-start(bf16[512,16]{0,1:T(8,128)(2,1)} %copy-done.45) | copy-start | bytes 49156
  750.9 4.9 copy-start.42
  750.9 556.6 %reduce-scatter.15.cloned.1.call-start = ((), (), s32[]{:S(2)}) async-start(), calls=%async_computation.14 | async-start | bytes 2162688 | tf_op jit(solution)/shard_map/reduce_scatter | solution.py:209
  753.8 6.5 copy-start.21
  753.8 6.5 copy-start.23
  755.4 689.1 %reduce-scatter.17.cloned.1.call-start = ((), (), s32[]{:S(2)}) async-start(), calls=%async_computation.15 | async-start | bytes 2162688 | tf_op jit(solution)/shard_map/reduce_scatter | solution.py:210
  760.3 6.4 copy-start.2
  760.3 6.4 copy-start.36
  760.4 6.4 copy-start.57
  (13 other events, 18.8 us)
Sparse Core Ops, SparseCore 0:
  11.4 79.7 all-gather.12
  94.7 92.3 all-gather.14
  189.9 46.8 all-gather.24
  239.5 48.0 all-gather.20
  290.4 68.7 all-gather.10
  361.9 54.7 all-gather.16
  419.6 75.8 all-gather.18
  498.4 75.6 all-gather.22
  629.1 134.5 reduce-scatter.24
  765.7 131.5 reduce-scatter.22
  899.6 134.2 reduce-scatter.20
  1036.0 134.2 reduce-scatter.18
  1173.2 134.2 reduce-scatter.14
  1310.2 134.3 reduce-scatter.16
where the time goes:
time: 1460 us; the launch traced here: 1450 us
  waiting for transfers between devices  921 us (63%)
  blocking collectives  183 us (13%)
  matrix products  162 us (11%)
  local copies, waits for them, and re-layouts  134 us (9%)
  other arithmetic  35.4 us (2%)
  between operations  16 us (1%)
    unnamed x18, waiting for transfers between devices  400 us
    dot_general x43, matrix products, product(): return jnp.einsum(form, left, right, preferred_element_type=jnp.float32)  162 us
    reduce_scatter x1, waiting for transfers between devices, on_device(): lax.psum_scatter(feed_terms[2], 'fsdp', scatter_dimension=1, tiled=True)  137 us
    reduce_scatter x1, waiting for transfers between devices, on_device(): lax.psum_scatter(feed_terms[1], 'fsdp', scatter_dimension=2, tiled=True)  135 us
    unnamed x146, local copies, waits for them, and re-layouts  93.2 us
    all_gather x1, waiting for transfers between devices, on_device(): lax.all_gather(expand_weight, 'fsdp', axis=0, tiled=True)  72.8 us
    all_gather x1, waiting for transfers between devices, on_device(): lax.all_gather(input_weight, 'fsdp', axis=1, tiled=True)  68.4 us
    all_gather x1, blocking collectives, on_device(): lax.all_gather(expand_down, 'fsdp', axis=1, tiled=True)  53.9 us
  transfers between devices with their start and end apart: 14, of which 11 were waited for; matrix products, arithmetic and copies ran while one was open for 18% of the time, Pallas kernels for 0%

commit v1 on v0

v1 whole, which is shorter than its diff:
```python
import jax
import jax.numpy as jnp
from jax import lax
from jax.sharding import PartitionSpec as P

HEAD_DIM = 64
epsilon = 1e-12
low = jnp.bfloat16


def product(form, left, right):
    return jnp.einsum(form, left, right, preferred_element_type=jnp.float32)


def layer_norm(values, gains, shifts):
    average = jnp.mean(values, axis=-1, keepdims=True)
    centered = values - average
    spread = jnp.mean(centered * centered, axis=-1, keepdims=True)
    return centered * lax.rsqrt(spread + epsilon) * gains + shifts


def exact_gelu(values):
    return jax.nn.gelu(values, approximate=False)


def masked_scores(queries, key_rows, segment):
    scores = product("qhd,khd->hqk", queries, key_rows) * HEAD_DIM ** (-0.5)
    same_doc = segment[:, None] == segment[None, :]
    return jnp.where(same_doc[None], scores, -1000000000.0)


def heads(rows):
    return rows.reshape(rows.shape[0], -1, HEAD_DIM)


def attend_forward(queries, key_rows, value_rows, segment):
    masked = masked_scores(heads(queries), heads(key_rows), segment)
    largest = jnp.max(masked, axis=-1, keepdims=True)
    log_total = largest + jnp.log(jnp.sum(jnp.exp(masked - largest), axis=-1, keepdims=True))
    weights = jnp.exp(masked - log_total).astype(low)
    context = product("hqk,khd->qhd", weights, heads(value_rows))
    return context.reshape(queries.shape).astype(low), log_total


def attend_backward(queries, key_rows, value_rows, segment, log_total, context_back):
    scaling = HEAD_DIM ** (-0.5)
    masked = masked_scores(heads(queries), heads(key_rows), segment)
    weights = jnp.exp(masked - log_total)
    weights_back = product("qhd,khd->hqk", heads(context_back), heads(value_rows))
    row_dots = jnp.sum(weights * weights_back, axis=-1, keepdims=True)
    scores_back = (weights * (weights_back - row_dots)).astype(low)
    query_back = product("hqk,khd->qhd", scores_back, heads(key_rows)) * scaling
    key_back = product("hqk,qhd->khd", scores_back, heads(queries)) * scaling
    value_back = product("hqk,qhd->khd", weights.astype(low), heads(context_back))
    return tuple(g.reshape(queries.shape).astype(low) for g in (query_back, key_back, value_back))


def on_device(
    tokens,
    cotangent,
    segments,
    adapter_id,
    input_weight,
    output_weight,
    norm_gain,
    norm_shift,
    attention_down,
    attention_up,
    expand_weight,
    reduce_weight,
    expand_down,
    expand_up,
    reduce_down,
    reduce_up,
):
    devices = lax.axis_size("fsdp")
    tables, adapters, part, rank = attention_down.shape
    width = part * devices
    inner_width = reduce_weight.shape[0] * devices
    part_inner = reduce_weight.shape[0]
    lanes = adapters * rank
    x = tokens[0]
    length = x.shape[0]

    packed_attention = jnp.concatenate(
        [
            input_weight.transpose(1, 0, 2).reshape(part, 3 * width),
            output_weight,
            attention_down.transpose(2, 0, 1, 3).reshape(part, tables * lanes),
            attention_up.transpose(3, 0, 1, 2).reshape(part, tables * lanes),
            jnp.pad(
                jnp.concatenate([norm_gain, norm_shift], axis=0).T, ((0, 0), (0, lanes - 4))
            ),
        ],
        axis=1,
    )
    packed_expand = jnp.concatenate(
        [
            expand_weight,
            expand_down.transpose(1, 0, 2).reshape(part, lanes),
            reduce_up.transpose(2, 0, 1).reshape(part, lanes),
        ],
        axis=1,
    )
    packed_reduce = jnp.concatenate(
        [
            reduce_weight,
            reduce_down.transpose(1, 0, 2).reshape(part_inner, lanes),
            expand_up.transpose(2, 0, 1).reshape(part_inner, lanes),
        ],
        axis=1,
    )
    whole = lax.all_gather(packed_attention, "fsdp", axis=0, tiled=True)
    whole_expand = lax.all_gather(packed_expand, "fsdp", axis=0, tiled=True)
    whole_reduce = lax.all_gather(packed_reduce, "fsdp", axis=0, tiled=True)

    row = lax.broadcasted_iota(jnp.int32, (lanes, lanes), 0)
    col = lax.broadcasted_iota(jnp.int32, (lanes, lanes), 1)

    def picked(table, slot):
        choose = (
            (row // rank == adapter_id[0]) & (row % rank == col % rank) & (col // rank == slot)
        ).astype(low)
        return product("xa,ab->xb", table, choose).astype(low)

    off = 4 * width
    down = [
        picked(whole[:, off + t * lanes : off + (t + 1) * lanes], t) for t in range(tables)
    ]
    off = off + tables * lanes
    up = [picked(whole[:, off + t * lanes : off + (t + 1) * lanes], t) for t in range(tables)]
    off = off + tables * lanes
    norms = whole[:, off : off + 4].astype(jnp.float32).T
    gain_one, gain_two, shift_one, shift_two = norms[0], norms[1], norms[2], norms[3]
    down_in = down[0] + down[1] + down[2]
    w_in = [whole[:, t * width : (t + 1) * width] for t in range(3)]
    w_out = whole[:, 3 * width : 4 * width]

    inner_in = product("lx,xr->lr", x, down_in).astype(low)
    q, k, v = [
        (product("lx,xe->le", x, w_in[t]) + product("lr,er->le", inner_in, up[t])).astype(low)
        for t in range(3)
    ]
    segment = segments[0]
    context, log_total = attend_forward(q, k, v, segment)
    inner_out = product("lx,xr->lr", context, down[3]).astype(low)
    branch = product("lx,xe->le", context, w_out) + product("lr,er->le", inner_out, up[3])
    hidden_one = x.astype(jnp.float32) + branch
    normed, norm_one_back = jax.vjp(lambda h: layer_norm(h, gain_one, shift_one), hidden_one)
    normed_low = normed.astype(low)

    w_exp = whole_expand[:, :inner_width]
    w_red = whole_reduce[:, :width]
    exp_down = picked(whole_expand[:, inner_width : inner_width + lanes], 0)
    red_up = picked(whole_expand[:, inner_width + lanes :], 1)
    red_down = picked(whole_reduce[:, width : width + lanes], 1)
    exp_up = picked(whole_reduce[:, width + lanes :], 0)
    inner_exp = product("lx,xr->lr", normed_low, exp_down).astype(low)
    expanded = product("lx,xf->lf", normed_low, w_exp) + product("lr,fr->lf", inner_exp, exp_up)
    active, gelu_back = jax.vjp(exact_gelu, expanded)
    active_low = active.astype(low)
    inner_red = product("lf,fr->lr", active_low, red_down).astype(low)
    reduced = product("lf,fe->le", active_low, w_red) + product("lr,er->le", inner_red, red_up)
    hidden_two = normed + reduced
    output, norm_two_back = jax.vjp(lambda h: layer_norm(h, gain_two, shift_two), hidden_two)

    two_back = norm_two_back(cotangent[0].astype(jnp.float32))[0]
    reduced_back = two_back.astype(low)
    inner_red_back = product("le,er->lr", reduced_back, red_up).astype(low)
    active_back = product("le,fe->lf", reduced_back, w_red) + product(
        "lr,fr->lf", inner_red_back, red_down
    )
    expanded_back = gelu_back(active_back)[0].astype(low)
    inner_exp_back = product("lf,fr->lr", expanded_back, exp_up).astype(low)
    normed_back = (
        two_back
        + product("lf,xf->lx", expanded_back, w_exp)
        + product("lr,xr->lx", inner_exp_back, exp_down)
    )
    grad_feed = product("lx,lr->xr", normed_low, inner_exp_back) + product(
        "lx,lr->xr", reduced_back, inner_red
    )
    grad_inner = product("lf,lr->fr", expanded_back, inner_exp) + product(
        "lf,lr->fr", active_low, inner_red_back
    )

    one_back = norm_one_back(normed_back)[0]
    branch_back = one_back.astype(low)
    inner_out_back = product("le,er->lr", branch_back, up[3]).astype(low)
    context_back = (
        product("le,xe->lx", branch_back, w_out) + product("lr,xr->lx", inner_out_back, down[3])
    ).astype(low)
    backs = attend_backward(q, k, v, segment, log_total, context_back)
    inner_in_back = sum(product("le,er->lr", backs[t], up[t]) for t in range(3)).astype(low)
    tokens_back = (
        one_back
        + sum(product("le,xe->lx", backs[t], w_in[t]) for t in range(3))
        + product("lr,xr->lx", inner_in_back, down_in)
    )
    grad_down = product("lx,lr->xr", x, inner_in_back) + product(
        "lx,lr->xr", context, inner_out_back
    )

    def only(inner, slot):
        lane = lax.broadcasted_iota(jnp.int32, inner.shape, 1)
        return jnp.where(lane // rank == slot, inner, jnp.zeros_like(inner))

    grad_up = (
        sum(product("le,lr->er", backs[t], only(inner_in, t)) for t in range(3))
        + product("le,lr->er", branch_back, inner_out)
    )
    half = tables * rank
    chosen = (jnp.arange(adapters, dtype=jnp.int32) == adapter_id[0]).astype(low)
    fold = part_inner // part
    sent = jnp.concatenate(
        [
            grad_down[:, :half].reshape(devices, part, half),
            grad_up[:, :half].reshape(devices, part, half),
            grad_feed[:, : 2 * rank].reshape(devices, part, 2 * rank),
            grad_inner[:, : 2 * rank]
            .reshape(devices, fold, part, 2 * rank)
            .transpose(0, 2, 1, 3)
            .reshape(devices, part, fold * 2 * rank),
        ],
        axis=2,
    ).astype(low)
    sent = jnp.concatenate(
        [sent, jnp.broadcast_to(chosen, (devices, part, adapters))], axis=2
    )
    got = lax.all_to_all(sent, "fsdp", 0, 0, tiled=True)
    who = got[:, 0, -adapters:]
    total = product("sa,sxc->axc", who, got[:, :, :-adapters])
    down_grad = total[:, :, :half].reshape(adapters, part, tables, rank).transpose(2, 0, 1, 3)
    up_grad = total[:, :, half : 2 * half].reshape(adapters, part, tables, rank)
    up_grad = up_grad.transpose(2, 0, 3, 1)
    base = 2 * half
    expand_down_grad = total[:, :, base : base + rank]
    reduce_up_grad = total[:, :, base + rank : base + 2 * rank].transpose(0, 2, 1)
    inner_total = (
        total[:, :, base + 2 * rank :]
        .reshape(adapters, part, fold, 2 * rank)
        .transpose(0, 2, 1, 3)
        .reshape(adapters, part_inner, 2 * rank)
    )
    expand_up_grad = inner_total[:, :, :rank].transpose(0, 2, 1)
    reduce_down_grad = inner_total[:, :, rank:]
    return (
        output.astype(low)[None],
        tokens_back[None],
        down_grad,
        up_grad,
        expand_down_grad,
        expand_up_grad,
        reduce_down_grad,
        reduce_up_grad,
    )


def solution(mesh):
    placed = (
        P("fsdp", None, None),
        P("fsdp", None, None),
        P("fsdp", None),
        P("fsdp"),
        P(None, "fsdp", None),
        P("fsdp", None),
        P(None, "fsdp"),
        P(None, "fsdp"),
        P(None, None, "fsdp", None),
        P(None, None, None, "fsdp"),
        P("fsdp", None),
        P("fsdp", None),
        P(None, "fsdp", None),
        P(None, None, "fsdp"),
        P(None, "fsdp", None),
        P(None, None, "fsdp"),
    )
    return jax.shard_map(
        on_device,
        mesh=mesh,
        in_specs=placed,
        out_specs=(
            P("fsdp", None, None),
            P("fsdp", None, None),
            P(None, None, "fsdp", None),
            P(None, None, None, "fsdp"),
            P(None, "fsdp", None),
            P(None, None, "fsdp"),
            P(None, "fsdp", None),
            P(None, None, "fsdp"),
        ),
        check_vma=False,
    )
```

time: 1460 us -> 537 us (0.37)
  waiting for transfers between devices: 921 us -> 250 us
  blocking collectives: 183 us -> 0 us
  local copies, waits for them, and re-layouts: 134 us -> 36.2 us
  matrix products: 162 us -> 184 us
    unnamed x18 -> x3, waiting for transfers between devices: 400 us -> 0.05 us
    reduce_scatter x2 -> x0, waiting for transfers between devices: 272 us -> none  [the longest x1 137 us: on_device(): lax.psum_scatter(feed_terms[2], 'fsdp', scatter_dimension=1, tiled=True)]
    all_gather x4 -> x0, blocking collectives: 183 us -> none  [the longest x1 53.9 us: on_device(): lax.all_gather(expand_down, 'fsdp', axis=1, tiled=True)]
    unnamed x146 -> x111, local copies, waits for them, and re-layouts: 93.2 us -> 7.19 us
    dot_general x43 -> x61, matrix products: 162 us -> 184 us  [product(): return jnp.einsum(form, left, right, preferred_element_type=jnp.float32)]
    all_gather x3 -> x0, local copies, waits for them, and re-layouts: 20.1 us -> none  [the longest x1 9.29 us: on_device(): lax.all_gather(attention_down, 'fsdp', axis=2, tiled=True)]
    all_gather x8 -> x3, waiting for transfers between devices: 249 us -> 241 us  [the longest x1 85.9 us: on_device(): whole = lax.all_gather(packed_attention, 'fsdp', axis=0, tiled=True)]
  transfers between devices with their start and end apart: 14 -> 4, of which waited for: 11 -> 4; matrix products, arithmetic and copies ran while one was open for 18% -> 5% of each run, Pallas kernels for 0% -> 0%
where the time goes in v1:
time: 537 us; the launch traced here: 530 us
  waiting for transfers between devices  250 us (47%)
  matrix products  184 us (34%)
  other arithmetic  40.2 us (7%)
  local copies, waits for them, and re-layouts  36.2 us (7%)
  between operations  15.8 us (3%)
    dot_general x61, matrix products, product(): return jnp.einsum(form, left, right, preferred_element_type=jnp.float32)  184 us
    all_gather x1, waiting for transfers between devices, on_device(): whole = lax.all_gather(packed_attention, 'fsdp', axis=0, tiled=True)  85.9 us
    all_gather x1, waiting for transfers between devices, on_device(): whole_reduce = lax.all_gather(packed_reduce, 'fsdp', axis=0, tiled=True)  84.2 us
    all_gather x1, waiting for transfers between devices, on_device(): whole_expand = lax.all_gather(packed_expand, 'fsdp', axis=0, tiled=True)  70.8 us
    convert_element_type x1, other arithmetic, attend_backward(): scores_back = (weights * (weights_back - row_dots)).astype(low)  12.3 us
  transfers between devices with their start and end apart: 4, of which 4 were waited for; matrix products, arithmetic and copies ran while one was open for 5% of the time, Pallas kernels for 0%

profile of v1, /device:TPU:0, one launch (start us, length us, event | category | flops | bytes accessed | tf_op | source)
XLA Modules:
  0.0 529.7 jit_solution(7589073646556555256)
XLA Ops:
  9.0 1.7 pad_maximum_fusion.1
  12.5 1.7 pad_maximum_fusion
  21.9 70.8 %all-gather.6.cloned.1.call-done = bf16[1024,4352]{1,0:T(8,128)(2,1)} async-done(((bf16[32,4352]{1,0:T(8,128)(2,1)}), bf16[1024,4352]{1,0:T(8,128)(2,1)}) %all-gather.6.cloned.1.call-update) | async-done | bytes 8912912 | tf_op jit(solution)/shard_map/all_gather | solution.py:114
  92.7 2.0 convolution_convert_fusion.5
  94.7 2.0 convolution_convert_fusion.4
  96.7 84.2 %all-gather.8.cloned.1.call-done = bf16[4096,1280]{1,0:T(8,128)(2,1)} async-done(((bf16[128,1280]{1,0:T(8,128)(2,1)}), bf16[4096,1280]{1,0:T(8,128)(2,1)}) %all-gather.8.cloned.1.call-update) | async-done | bytes 10485776 | tf_op jit(solution)/shard_map/all_gather | solution.py:115
  180.9 1.8 convolution_convert_fusion.1
  182.7 1.8 convolution_convert_fusion
  184.5 85.9 %all-gather.4.cloned.1.call-done = bf16[1024,5248]{1,0:T(8,128)(2,1)} async-done(((bf16[32,5248]{1,0:T(8,128)(2,1)}), bf16[1024,5248]{1,0:T(8,128)(2,1)}) %all-gather.4.cloned.1.call-update) | async-done | bytes 10747920 | tf_op jit(solution)/shard_map/all_gather | solution.py:113
  270.4 1.3 convolution_convert_fusion.11
  271.7 1.3 convolution_convert_fusion.12
  273.0 1.3 fusion.40
  275.6 2.9 fusion.28
  278.5 1.3 convolution_convert_fusion.8
  281.0 3.3 fusion.32
  284.3 1.3 convolution_convert_fusion.9
  286.3 8.2 %fusion = (f32[16,512]{1,0:T(8,128)}, f32[16,512,512]{1,2,0:T(8,128)}) fusion(pred[512,512]{0,1:T(8,128)(4,1)S(1)} %broadcast_compare_fusion, bf16[512,16,64]{0,2,1:T(8,128)(2,1)S(1)} %bitcast.208, bf16[512,16,64]{0,2,1:T(8,128)(2,1)S(1)} %bitcast.203), kind=kOutput, calls=%fused_computation.5 | convolution fusion | flops 549445632 | bytes 19169280 | tf_op jit(solution)/shard_map/qhd,khd->hqk/dot_general | solution.py:12
  294.5 9.8 %exponential_reduce_fusion = f32[16,512]{1,0:T(8,128)} fusion(f32[16,512,512]{1,2,0:T(8,128)} %get-tuple-element.62, f32[16,512]{1,0:T(8,128)} %get-tuple-element.61, pred[512,512]{0,1:T(8,128)(4,1)S(1)} %broadcast_compare_fusion), kind=kLoop, calls=%fused_computation.3 | loop fusion | flops 16769024 | bytes 17104896 | tf_op jit(solution)/shard_map/reduce_sum | solution.py:39
  305.1 2.9 fusion.36
  308.0 1.3 convolution_convert_fusion.10
  309.8 8.9 %convolution_convert_fusion.3 = bf16[16,64,512]{2,1,0:T(8,128)(2,1)S(1)} fusion(bf16[512,16,64]{0,2,1:T(8,128)(2,1)S(1)} %bitcast.216, f32[16,512,512]{1,2,0:T(8,128)} %get-tuple-element.62, f32[16,512]{1,0:T(8,128)S(1)} %log_add_fusion, pred[512,512]{0,1:T(8,128)(4,1)S(1)} %broadcast_compare_fusion), kind=kOutput, calls=%fused_computation.79 | convolution fusion | flops 554172416 | bytes 19169280 | tf_op jit(solution)/shard_map/hqk,khd->qhd/dot_general | solution.py:12
  318.7 1.5 convolution_convert_fusion.7
  320.9 2.9 fusion.24
  323.9 1.3 convolution_convert_fusion.6
  329.1 10.2 %fusion.14 = f32[512,4096]{1,0:T(8,128)} fusion(bf16[512,1024]{1,0:T(8,128)(2,1)S(1)} %fusion.38, bf16[1024,4352]{1,0:T(8,128)(2,1)} %all-gather.6.cloned.1.call-done), kind=kOutput, calls=%fused_computation.30 | convolution fusion | flops 4294967296 | bytes 17825792 | tf_op jit(solution)/shard_map/lx,xf->lf/dot_general | solution.py:12
  339.3 21.6 %multiply_convert_fusion.1 = (bf16[512,4096]{1,0:T(8,128)(2,1)S(1)}, f32[512,4096]{1,0:T(8,128)S(1)}, f32[512,4096]{1,0:T(8,128)}) fusion(f32[512,4096]{1,0:T(8,128)} %fusion.14, bf16[512,128]{1,0:T(8,128)(2,1)S(1)} %convolution_convert_fusion.18, bf16[4096,128]{1,0:T(8,128)(2,1)S(1)} %convolution_convert_fusion.1), kind=kOutput, calls=%fused_computation.10 | convolution fusion | flops 675282944 | bytes 30539776 | tf_op jit(solution)/shard_map/lr,fr->lf/dot_general | solution.py:12
  362.3 7.1 %fusion.10 = f32[512,1024]{1,0:T(8,128)S(1)} fusion(bf16[512,4096]{1,0:T(8,128)(2,1)S(1)} %get-tuple-element.50, bf16[4096,1280]{1,0:T(8,128)(2,1)} %all-gather.8.cloned.1.call-done), kind=kOutput, calls=%fused_computation.26 | convolution fusion | flops 4294967296 | bytes 14680064 | tf_op jit(solution)/shard_map/lf,fe->le/dot_general | solution.py:12
  370.9 1.9 fusion.142
  374.6 2.1 fusion.154
  376.6 10.2 %fusion.8 = f32[512,4096]{1,0:T(8,128)} fusion(bf16[512,1024]{1,0:T(8,128)(2,1)S(1)} %add_convert_fusion.4, bf16[4096,1280]{1,0:T(8,128)(2,1)} %all-gather.8.cloned.1.call-done), kind=kOutput, calls=%fused_computation.24 | convolution fusion | flops 4294967296 | bytes 17825792 | tf_op jit(solution)/shard_map/le,fe->lf/dot_general | solution.py:12
  386.9 8.0 %add_convert_fusion = bf16[512,4096]{1,0:T(8,128)(2,1)S(1)} fusion(f32[512,4096]{1,0:T(8,128)S(1)} %get-tuple-element.51, f32[512,4096]{1,0:T(8,128)} %fusion.8, f32[512,4096]{1,0:T(8,128)} %get-tuple-element.65, bf16[512,128]{1,0:T(8,128)(2,1)S(1)} %convolution_convert_fusion.17, bf16[4096,128]{1,0:T(8,128)(2,1)S(1)} %convolution_convert_fusion), kind=kOutput, calls=%fused_computation.9 | convolution fusion | flops 568328192 | bytes 30539776 | tf_op jit(solution)/shard_map/lr,fr->lf/dot_general | solution.py:12
  394.9 2.1 fusion.153
  399.4 7.2 %fusion.12 = f32[512,1024]{1,0:T(8,128)S(1)} fusion(bf16[512,4096]{1,0:T(8,128)(2,1)S(1)} %add_convert_fusion, bf16[1024,4352]{1,0:T(8,128)(2,1)} %all-gather.6.cloned.1.call-done), kind=kOutput, calls=%fused_computation.28 | convolution fusion | flops 4294967296 | bytes 14680064 | tf_op jit(solution)/shard_map/lf,xf->lx/dot_general | solution.py:12
  409.4 3.0 fusion.22
  412.4 1.4 add_convert_fusion.1
  413.8 2.3 copy.124
  416.1 12.4 %multiply_reduce_fusion = (f32[16,512]{1,0:T(8,128)S(1)}, f32[16,512,512]{1,2,0:T(8,128)}) fusion(f32[16,512,512]{1,2,0:T(8,128)} %get-tuple-element.62, f32[16,512]{1,0:T(8,128)S(1)} %copy-done.37, pred[512,512]{0,1:T(8,128)(4,1)S(1)} %copy-done.10, bf16[512,16,64]{0,2,1:T(8,128)(2,1)} %bitcast.218, bf16[512,16,64]{0,2,1:T(8,128)(2,1)S(1)} %bitcast.217), kind=kOutput, calls=%fused_computation.1 | convolution fusion | flops 557834240 | bytes 35979264 | tf_op jit(solution)/shard_map/qhd,khd->hqk/dot_general | solution.py:12
  428.5 12.3 %multiply_convert_fusion = bf16[16,512,512]{1,2,0:T(8,128)(2,1)S(1)} fusion(f32[16,512,512]{1,2,0:T(8,128)} %get-tuple-element.71, f32[16,512,512]{1,2,0:T(8,128)} %get-tuple-element.62, f32[16,512]{1,0:T(8,128)S(1)} %get-tuple-element.70, f32[16,512]{1,0:T(8,128)S(1)} %copy-done.37, pred[512,512]{0,1:T(8,128)(4,1)S(1)} %copy-done.10), kind=kLoop, calls=%fused_computation | loop fusion | flops 25165824 | bytes 42270720 | tf_op jit(solution)/shard_map/convert_element_type | solution.py:51
  440.8 3.6 multiply_convert_fusion.2
  444.5 1.5 multiply_convert_fusion.3
  447.2 9.3 %convolution_convert_fusion.2 = bf16[16,64,512]{2,1,0:T(8,128)(2,1)} fusion(bf16[512,16,64]{0,2,1:T(8,128)(2,1)S(1)} %bitcast.219, f32[16,512,512]{1,2,0:T(8,128)} %get-tuple-element.62, f32[16,512]{1,0:T(8,128)S(1)} %copy-done.38, pred[512,512]{0,1:T(8,128)(4,1)S(1)} %copy-done.10), kind=kOutput, calls=%fused_computation.78 | convolution fusion | flops 554172416 | bytes 19169280 | tf_op jit(solution)/shard_map/hqk,qhd->khd/dot_general | solution.py:12
  456.6 1.3 fusion.72
  459.0 1.3 fusion.149
  460.3 1.9 fusion.52
  462.3 2.7 reshape.199
  464.9 3.5 copy.130
  468.4 2.6 reshape.200
  471.0 1.6 fusion.74
  472.6 1.7 copy.148
  474.3 1.7 fusion.70
  476.0 1.7 fusion.68
  479.6 1.7 convolution_add_fusion.2
  481.4 1.7 fusion.41
  483.1 1.6 convolution_bitcast_fusion
  484.7 1.6 fusion.54
  487.4 1.4 broadcast_in_dim.54
  488.8 2.4 concatenate.22
  491.2 3.3 all-to-all-start
  494.6 3.3 fusion.26
  497.9 2.9 fusion.30
  500.8 2.9 fusion.34
  503.7 2.0 add_bitcast_fusion
  505.7 9.4 %all-to-all-done = bf16[32,32,296]{2,1,0:T(8,128)(2,1)} async-done(((bf16[32,32,296]{2,1,0:T(8,128)(2,1)}), bf16[32,32,296]{2,1,0:T(8,128)(2,1)}, u32[]{:S(2)}, u32[]{:S(2)}) %all-to-all-start) | async-done | bytes 606240 | tf_op jit(solution)/shard_map/all_to_all | solution.py:230
  516.1 1.5 fusion.50
  (178 shorter events, 40.5 us)
Async XLA Ops:
  7.2 267.9 %copy-start.4 = (bf16[1,512,1024]{2,1,0:T(8,128)(2,1)S(1)}, bf16[1,512,1024]{2,1,0:T(8,128)(2,1)}, u32[]{:S(2)}) copy-start(bf16[1,512,1024]{2,1,0:T(8,128)(2,1)} %param.16) | copy-start | bytes 3145732
  7.2 85.5 %all-gather.6.cloned.1.call-start = ((), (), s32[]{:S(2)}) async-start(), calls=%async_computation.2 | async-start | bytes 9191424 | tf_op jit(solution)/shard_map/all_gather | solution.py:114
  10.7 170.2 %all-gather.8.cloned.1.call-start = ((), (), s32[]{:S(2)}) async-start(), calls=%async_computation.3 | async-start | bytes 10813440 | tf_op jit(solution)/shard_map/all_gather | solution.py:115
  14.2 256.2 %all-gather.4.cloned.1.call-start = ((), (), s32[]{:S(2)}) async-start(), calls=%async_computation.1 | async-start | bytes 11083776 | tf_op jit(solution)/shard_map/all_gather | solution.py:113
  18.9 0.7 copy-start.35
  20.9 303.0 %copy-start.39 = (pred[128]{0:T(512)(128)(4,1)}, pred[128]{0:T(512)(128)(4,1)S(1)}, u32[]{:S(2)}) copy-start(pred[128]{0:T(512)(128)(4,1)S(1)} %get-tuple-element.73) | copy-start | bytes 388
  20.9 252.1 %copy-start.45 = (s32[128]{0:T(128)}, s32[128]{0:T(128)S(1)}, u32[]{:S(2)}) copy-start(s32[128]{0:T(128)S(1)} %get-tuple-element.75) | copy-start | bytes 1540
  20.9 303.0 %copy-start.41 = (s32[128]{0:T(128)}, s32[128]{0:T(128)S(1)}, u32[]{:S(2)}) copy-start(s32[128]{0:T(128)S(1)} %get-tuple-element.74) | copy-start | bytes 1540
  20.9 252.1 %copy-start.48 = (s32[128]{0:T(128)}, s32[128]{0:T(128)S(1)}, u32[]{:S(2)}) copy-start(s32[128]{0:T(128)S(1)} %get-tuple-element.76) | copy-start | bytes 1540
  20.9 303.0 %copy-start.43 = (s32[128]{0:T(128)}, s32[128]{0:T(128)S(1)}, u32[]{:S(2)}) copy-start(s32[128]{0:T(128)S(1)} %get-tuple-element.77) | copy-start | bytes 1540
  21.9 287.9 %copy-start.9 = (pred[512,512]{0,1:T(8,128)(4,1)}, pred[512,512]{0,1:T(8,128)(4,1)S(1)}, u32[]{:S(2)}) copy-start(pred[512,512]{0,1:T(8,128)(4,1)S(1)} %broadcast_compare_fusion) | copy-start | bytes 786436
  274.4 0.7 copy-start.24
  275.1 3.4 copy-start.46
  275.1 3.5 copy-start.49
  275.6 33.8 %copy-start.11 = (bf16[128,512]{1,0:T(8,128)(2,1)}, bf16[128,512]{1,0:T(8,128)(2,1)S(1)}, u32[]{:S(2)}) copy-start(bf16[128,512]{1,0:T(8,128)(2,1)S(1)} %convolution_convert_fusion.20) | copy-start | bytes 393220
  279.9 0.7 copy-start.22
  281.0 13.5 %copy-start = (bf16[512,1024]{0,1:T(8,128)(2,1)}, bf16[512,1024]{0,1:T(8,128)(2,1)S(1)}, u32[]{:S(2)}) copy-start(bf16[512,1024]{0,1:T(8,128)(2,1)S(1)} %fusion.19) | copy-start | bytes 3145732
  285.6 0.7 copy-start.27
  286.3 8.2 %copy-start.2 = (bf16[512,1024]{0,1:T(8,128)(2,1)}, bf16[512,1024]{0,1:T(8,128)(2,1)S(1)}, u32[]{:S(2)}) copy-start(bf16[512,1024]{0,1:T(8,128)(2,1)S(1)} %fusion.20) | copy-start | bytes 3145732
  304.3 3.7 copy-start.47
  304.3 3.7 copy-start.50
  305.1 13.6 %copy-start.36 = (f32[16,512]{1,0:T(8,128)}, f32[16,512]{1,0:T(8,128)S(1)}, u32[]{:S(2)}) copy-start(f32[16,512]{1,0:T(8,128)S(1)} %log_add_fusion) | copy-start | bytes 98308
  309.3 9.3 %copy-start.26 = (bf16[1024,128]{1,0:T(8,128)(2,1)}, bf16[1024,128]{1,0:T(8,128)(2,1)S(1)}, u32[]{:S(2)}) copy-start(bf16[1024,128]{1,0:T(8,128)(2,1)S(1)} %convolution_convert_fusion.10) | copy-start | bytes 786436
  309.8 8.9 %copy-start.13 = (bf16[512,1024]{0,1:T(8,128)(2,1)}, bf16[512,1024]{0,1:T(8,128)(2,1)S(1)}, u32[]{:S(2)}) copy-start(bf16[512,1024]{0,1:T(8,128)(2,1)S(1)} %fusion.21) | copy-start | bytes 3145732
  318.7 9.6 %copy-start.5 = (bf16[16,64,512]{2,1,0:T(8,128)(2,1)}, bf16[16,64,512]{2,1,0:T(8,128)(2,1)S(1)}, u32[]{:S(2)}) copy-start(bf16[16,64,512]{2,1,0:T(8,128)(2,1)S(1)} %convolution_convert_fusion.3) | copy-start | bytes 3145732
  320.2 0.7 copy-start.30
  320.9 7.7 %copy-start.20 = (bf16[512,128]{1,0:T(8,128)(2,1)}, bf16[512,128]{1,0:T(8,128)(2,1)S(1)}, u32[]{:S(2)}) copy-start(bf16[512,128]{1,0:T(8,128)(2,1)S(1)} %convolution_convert_fusion.19) | copy-start | bytes 393220
  323.9 4.8 copy-start.29
  325.3 14.1 %copy-start.32 = (bf16[1024,128]{1,0:T(8,128)(2,1)}, bf16[1024,128]{1,0:T(8,128)(2,1)S(1)}, u32[]{:S(2)}) copy-start(bf16[1024,128]{1,0:T(8,128)(2,1)S(1)} %convolution_convert_fusion.6) | copy-start | bytes 786436
  362.2 7.2 %copy-start.34 = (bf16[1024,128]{1,0:T(8,128)(2,1)S(1)}, bf16[1024,128]{1,0:T(8,128)(2,1)}, u32[]{:S(2)}) copy-start(bf16[1024,128]{1,0:T(8,128)(2,1)} %convolution_convert_fusion.4) | copy-start | bytes 786436
  362.2 8.0 %copy-start.17 = (bf16[1,512,1024]{2,1,0:T(8,128)(2,1)S(1)}, bf16[1,512,1024]{2,1,0:T(8,128)(2,1)}, u32[]{:S(2)}) copy-start(bf16[1,512,1024]{2,1,0:T(8,128)(2,1)} %param.17) | copy-start | bytes 3145732
  406.6 1.8 copy-start.33
  408.2 4.2 copy-start.31
  408.4 1.0 copy-start.7
  409.4 3.0 copy-start.18
  409.4 6.7 %copy-start.10 = (pred[512,512]{0,1:T(8,128)(4,1)S(1)}, pred[512,512]{0,1:T(8,128)(4,1)}, u32[]{:S(2)}) copy-start(pred[512,512]{0,1:T(8,128)(4,1)} %copy-done.9) | copy-start | bytes 786436
  409.4 6.7 %copy-start.14 = (bf16[512,1024]{0,1:T(8,128)(2,1)S(1)}, bf16[512,1024]{0,1:T(8,128)(2,1)}, u32[]{:S(2)}) copy-start(bf16[512,1024]{0,1:T(8,128)(2,1)} %copy-done.13) | copy-start | bytes 3145732
  409.4 6.7 %copy-start.37 = (f32[16,512]{1,0:T(8,128)S(1)}, f32[16,512]{1,0:T(8,128)}, u32[]{:S(2)}) copy-start(f32[16,512]{1,0:T(8,128)} %copy-done.36) | copy-start | bytes 98308
  428.5 12.3 %copy-start.3 = (bf16[512,1024]{0,1:T(8,128)(2,1)S(1)}, bf16[512,1024]{0,1:T(8,128)(2,1)}, u32[]{:S(2)}) copy-start(bf16[512,1024]{0,1:T(8,128)(2,1)} %copy-done.2) | copy-start | bytes 3145732
  440.8 3.6 copy-start.1
  444.5 1.5 copy-start.8
  444.5 1.5 copy-start.21
  444.5 2.7 copy-start.15
  444.5 2.7 copy-start.38
  447.1 9.4 %copy-start.12 = (bf16[128,512]{1,0:T(8,128)(2,1)S(1)}, bf16[128,512]{1,0:T(8,128)(2,1)}, u32[]{:S(2)}) copy-start(bf16[128,512]{1,0:T(8,128)(2,1)} %copy-done.11) | copy-start | bytes 393220
  447.1 9.4 %copy-start.40 = (pred[128]{0:T(512)(128)(4,1)S(1)}, pred[128]{0:T(512)(128)(4,1)}, u32[]{:S(2)}) copy-start(pred[128]{0:T(512)(128)(4,1)} %copy-done.39) | copy-start | bytes 388
  447.1 9.4 %copy-start.42 = (s32[128]{0:T(128)S(1)}, s32[128]{0:T(128)}, u32[]{:S(2)}) copy-start(s32[128]{0:T(128)} %copy-done.41) | copy-start | bytes 1540
  447.2 9.4 %copy-start.44 = (s32[128]{0:T(128)S(1)}, s32[128]{0:T(128)}, u32[]{:S(2)}) copy-start(s32[128]{0:T(128)} %copy-done.43) | copy-start | bytes 1540
  447.2 10.7 %copy-start.28 = (bf16[1024,128]{1,0:T(8,128)(2,1)S(1)}, bf16[1024,128]{1,0:T(8,128)(2,1)}, u32[]{:S(2)}) copy-start(bf16[1024,128]{1,0:T(8,128)(2,1)} %copy-done.27) | copy-start | bytes 786436
  447.2 11.9 %copy-start.6 = (bf16[16,64,512]{2,1,0:T(8,128)(2,1)S(1)}, bf16[16,64,512]{2,1,0:T(8,128)(2,1)}, u32[]{:S(2)}) copy-start(bf16[16,64,512]{2,1,0:T(8,128)(2,1)} %copy-done.5) | copy-start | bytes 3145732
  447.2 11.9 %copy-start.19 = (bf16[512,128]{1,0:T(8,128)(2,1)S(1)}, bf16[512,128]{1,0:T(8,128)(2,1)}, u32[]{:S(2)}) copy-start(bf16[512,128]{1,0:T(8,128)(2,1)} %copy-done.18) | copy-start | bytes 393220
  456.5 23.1 %copy-start.23 = (bf16[1024,128]{1,0:T(8,128)(2,1)S(1)}, bf16[1024,128]{1,0:T(8,128)(2,1)}, u32[]{:S(2)}) copy-start(bf16[1024,128]{1,0:T(8,128)(2,1)} %copy-done.22) | copy-start | bytes 786436
  491.2 23.9 %all-to-all-start = ((bf16[32,32,296]{2,1,0:T(8,128)(2,1)}), bf16[32,32,296]{2,1,0:T(8,128)(2,1)}, u32[]{:S(2)}, u32[]{:S(2)}) async-start(bf16[32,32,296]{2,1,0:T(8,128)(2,1)} %concatenate.22), calls=%async_computation | async-start | bytes 1572864 | tf_op jit(solution)/shard_map/all_to_all | solution.py:230
  494.5 6.2 %copy-start.16 = (bf16[16,64,512]{2,1,0:T(8,128)(2,1)S(1)}, bf16[16,64,512]{2,1,0:T(8,128)(2,1)}, u32[]{:S(2)}) copy-start(bf16[16,64,512]{2,1,0:T(8,128)(2,1)} %convolution_convert_fusion.2) | copy-start | bytes 3145732
  497.8 5.8 %copy-start.25 = (bf16[1024,128]{1,0:T(8,128)(2,1)S(1)}, bf16[1024,128]{1,0:T(8,128)(2,1)}, u32[]{:S(2)}) copy-start(bf16[1024,128]{1,0:T(8,128)(2,1)} %copy-done.24) | copy-start | bytes 786436
Sparse Core Ops, SparseCore 0:
  10.8 81.8 all-gather.5
  96.1 84.7 all-gather.7
  184.4 85.9 all-gather.3

commit v2 on v1

v2 whole, which is shorter than its diff:
```python
import jax
import jax.numpy as jnp
from jax import lax
from jax.experimental import pallas as pl
from jax.experimental.pallas import tpu as pltpu
from jax.sharding import PartitionSpec as P

HEAD_DIM = 64
epsilon = 1e-12
low = jnp.bfloat16
wide = jnp.float32
scaling = HEAD_DIM ** (-0.5)
far = -1000000000.0


def nn(left, right):
    return lax.dot_general(left, right, (((1,), (0,)), ((), ())), preferred_element_type=wide)


def nt(left, right):
    return lax.dot_general(left, right, (((1,), (1,)), ((), ())), preferred_element_type=wide)


def tn(left, right):
    return lax.dot_general(left, right, (((0,), (0,)), ((), ())), preferred_element_type=wide)


def lane_of(values):
    return lax.broadcasted_iota(jnp.int32, values.shape, 1)


def only(values, first, last):
    lane = lane_of(values)
    return jnp.where((lane >= first) & (lane < last), values, jnp.zeros_like(values))


def normalize(values):
    average = jnp.mean(values, axis=-1, keepdims=True)
    centered = values - average
    spread = jnp.mean(centered * centered, axis=-1, keepdims=True)
    scale = lax.rsqrt(spread + epsilon)
    return centered * scale, scale


def normalize_back(grads, normal, scale):
    return scale * (
        grads
        - jnp.mean(grads, axis=-1, keepdims=True)
        - normal * jnp.mean(grads * normal, axis=-1, keepdims=True)
    )


def tile_of(width):
    return min(256, width)


def attend_kernel(
    rank,
    x_ref,
    seg_row_ref,
    seg_col_ref,
    sel_ref,
    whole_ref,
    q_ref,
    k_ref,
    v_ref,
    context_ref,
    lse_ref,
    inner_ref,
    tab_ref,
    hidden_ref,
    w_ref,
    raw_ref,
    mask_ref,
    stat_ref,
    sems,
):
    length, width = x_ref.shape
    lanes = inner_ref.shape[1]
    raw_width = raw_ref.shape[1]
    half = raw_width // 2

    def fetch(t):
        if t == 4:
            return pltpu.make_async_copy(
                whole_ref.at[:, pl.ds(4 * width, raw_width)], raw_ref, sems.at[t]
            )
        return pltpu.make_async_copy(
            whole_ref.at[:, pl.ds(t * width, width)], w_ref.at[t], sems.at[t]
        )

    for t in (4, 0, 1, 2, 3):
        fetch(t).start()
    mask_ref[...] = (seg_col_ref[...] == seg_row_ref[...]).astype(wide)
    fetch(4).wait()
    tab_ref[:, :lanes] = nn(raw_ref[:, :half], sel_ref[...]).astype(low)
    tab_ref[:, lanes:] = nn(raw_ref[:, half:], sel_ref[...]).astype(low)
    inner_in = only(nn(x_ref[...], tab_ref[:, :lanes]).astype(low), 0, 3 * rank)
    tile = tile_of(width)
    for t, out in enumerate((q_ref, k_ref, v_ref)):
        fetch(t).wait()
        inner_t = only(inner_in, t * rank, (t + 1) * rank)

        @pl.loop(0, width // tile)
        def _(j, t=t, out=out, inner_t=inner_t):
            cols = pl.ds(pl.multiple_of(j * tile, tile), tile)
            out[:, cols] = (
                nn(x_ref[...], w_ref[t, :, cols]) + nt(inner_t, tab_ref[cols, lanes:])
            ).astype(low)

    pair = 2 * HEAD_DIM
    rows_at_once = min(256, length)
    stat_ref[...] = jnp.zeros_like(stat_ref)

    @pl.loop(0, width // pair)
    def _(p):
        cols = pl.ds(pl.multiple_of(p * pair, pair), pair)
        for r in range(0, length, rows_at_once):
            rows = pl.ds(r, rows_at_once)
            left = lax.broadcasted_iota(jnp.int32, (rows_at_once, pair), 1) < HEAD_DIM
            query = q_ref[rows, cols]
            both = []
            for h in range(2):
                mine = left if h == 0 else jnp.logical_not(left)
                scores = nt(jnp.where(mine, query, jnp.zeros_like(query)), k_ref[:, cols])
                masked = jnp.where(mask_ref[rows, :] > 0.5, scores * scaling, far)
                largest = jnp.max(masked, axis=-1, keepdims=True)
                grown = jnp.exp(masked - largest)
                total = jnp.sum(grown, axis=-1, keepdims=True)
                weights = (grown * (1.0 / total)).astype(low)
                both.append(nn(weights, v_ref[:, cols]))
                lane = lax.broadcasted_iota(jnp.int32, (rows_at_once, stat_ref.shape[1]), 1)
                stat_ref[rows, :] = jnp.where(
                    lane == 2 * p + h, largest + jnp.log(total), stat_ref[rows, :]
                )
            context_ref[rows, cols] = jnp.where(left, both[0], both[1]).astype(low)

    lse_ref[...] = stat_ref[...].T
    inner_out = only(
        nn(context_ref[...], tab_ref[:, :lanes]).astype(low), 3 * rank, 4 * rank
    )
    inner_ref[...] = inner_in + inner_out
    fetch(3).wait()

    @pl.loop(0, width // tile)
    def _(j):
        cols = pl.ds(pl.multiple_of(j * tile, tile), tile)
        hidden_ref[:, cols] = x_ref[:, cols].astype(wide) + (
            nn(context_ref[...], w_ref[3, :, cols]) + nt(inner_out, tab_ref[cols, lanes:])
        )


def feed_kernel(
    rank,
    hidden_ref,
    cot_ref,
    norms_ref,
    sel_exp_ref,
    sel_red_ref,
    exp_ref,
    red_ref,
    output_ref,
    back_ref,
    grad_w_ref,
    grad_f_ref,
    we_ref,
    wr_ref,
    raw_w_ref,
    raw_f_ref,
    tab_w_ref,
    tab_f_ref,
    low_ref,
    active_ref,
    slope_ref,
    sum_ref,
    two_ref,
    sems,
    sems_r,
    sems_f,
):
    length, width = hidden_ref.shape
    chunks, _, chunk = we_ref.shape
    inner_width = chunks * chunk
    lanes = tab_w_ref.shape[1]

    def fetch_e(j):
        return pltpu.make_async_copy(
            exp_ref.at[:, pl.ds(pl.multiple_of(j * chunk, chunk), chunk)], we_ref.at[j], sems.at[j]
        )

    def fetch_r(j):
        return pltpu.make_async_copy(
            red_ref.at[pl.ds(pl.multiple_of(j * chunk, chunk), chunk), pl.ds(0, width)],
            wr_ref.at[j],
            sems_r.at[j],
        )

    def fetch_f(j):
        return pltpu.make_async_copy(
            red_ref.at[
                pl.ds(pl.multiple_of(j * chunk, chunk), chunk), pl.ds(width, 2 * lanes)
            ],
            raw_f_ref.at[j],
            sems_f.at[j],
        )

    raw_copy = pltpu.make_async_copy(
        exp_ref.at[:, pl.ds(inner_width, 2 * lanes)], raw_w_ref, sems.at[chunks]
    )
    raw_copy.start()

    @pl.loop(0, chunks)
    def _(j):
        fetch_e(j).start()
        fetch_f(j).start()
        fetch_r(j).start()

    normal, _ = normalize(hidden_ref[...])
    normed = normal * norms_ref[0:1, :] + norms_ref[2:3, :]
    low_ref[...] = normed.astype(low)
    sum_ref[...] = normed
    raw_copy.wait()
    tab_w_ref[...] = nn(raw_w_ref[...], sel_exp_ref[...]).astype(low)
    inner_exp = only(nn(low_ref[...], tab_w_ref[...]).astype(low), 0, rank)

    def forward(j, inner_sum):
        fetch_f(j).wait()
        tab_f_ref[j] = nn(raw_f_ref[j], sel_red_ref[...]).astype(low)
        fetch_e(j).wait()
        expanded = nn(low_ref[...], we_ref[j]) + nt(inner_exp, tab_f_ref[j])
        share = 0.5 * (1.0 + lax.erf(expanded * (2.0 ** -0.5)))
        density = jnp.exp(-0.5 * expanded * expanded) * 0.3989422804014327
        slope_ref[j] = share + expanded * density
        active = (expanded * share).astype(low)
        active_ref[j] = active
        fetch_r(j).wait()
        sum_ref[...] += nn(active, wr_ref[j])
        return inner_sum + nn(active, tab_f_ref[j])

    inner_sum = lax.fori_loop(0, chunks, forward, jnp.zeros((length, lanes), wide))
    inner_red = only(inner_sum.astype(low), rank, 2 * rank)
    normal, scale = normalize(sum_ref[...] + nt(inner_red, tab_w_ref[...]))
    output_ref[...] = (normal * norms_ref[1:2, :] + norms_ref[3:4, :]).astype(low)
    two_back = normalize_back(cot_ref[...].astype(wide) * norms_ref[1:2, :], normal, scale)
    reduced_back = two_back.astype(low)
    two_ref[...] = reduced_back
    inner_red_back = only(nn(reduced_back, tab_w_ref[...]).astype(low), rank, 2 * rank)
    sum_ref[...] = two_back

    def backward(j, inner_sum):
        active_back = nt(two_ref[...], wr_ref[j]) + nt(inner_red_back, tab_f_ref[j])
        expanded_back = (active_back * slope_ref[j]).astype(low)
        sum_ref[...] += nt(expanded_back, we_ref[j])
        cols = pl.ds(pl.multiple_of(j * chunk, chunk), chunk)
        grad_f_ref[:, cols] = (
            tn(inner_exp, expanded_back) + tn(inner_red_back, active_ref[j])
        )[: 2 * rank].astype(low)
        return inner_sum + nn(expanded_back, tab_f_ref[j])

    inner_sum = lax.fori_loop(0, chunks, backward, jnp.zeros((length, lanes), wide))
    inner_exp_back = only(inner_sum.astype(low), 0, rank)
    grad_w_ref[...] = (
        (tn(inner_exp_back, low_ref[...]) + tn(inner_red, two_ref[...])).T.astype(low)
    )
    normal, scale = normalize(hidden_ref[...])
    normed_back = sum_ref[...] + nt(inner_exp_back, tab_w_ref[...])
    back_ref[...] = normalize_back(normed_back * norms_ref[0:1, :], normal, scale)


def attend_back_kernel(
    rank,
    x_ref,
    seg_row_ref,
    seg_col_ref,
    q_ref,
    k_ref,
    v_ref,
    context_ref,
    lse_ref,
    inner_ref,
    tab_ref,
    one_ref,
    whole_ref,
    out_ref,
    grad_ref,
    w_ref,
    mask_ref,
    low_ref,
    cback_ref,
    dq_ref,
    dk_ref,
    dv_ref,
    gt_ref,
    sems,
):
    length, width = x_ref.shape
    lanes = inner_ref.shape[1]

    def fetch(t):
        return pltpu.make_async_copy(
            whole_ref.at[:, pl.ds(t * width, width)], w_ref.at[t], sems.at[t]
        )

    for t in (3, 0, 1, 2):
        fetch(t).start()
    mask_ref[...] = (seg_col_ref[...] == seg_row_ref[...]).astype(wide)
    low_ref[...] = one_ref[...].astype(low)
    inner_out_back = only(
        nn(low_ref[...], tab_ref[:, lanes:]).astype(low), 3 * rank, 4 * rank
    )
    tile = tile_of(width)
    fetch(3).wait()

    @pl.loop(0, width // tile)
    def _(j):
        cols = pl.ds(pl.multiple_of(j * tile, tile), tile)
        cback_ref[:, cols] = (
            nt(low_ref[...], w_ref[3, cols, :]) + nt(inner_out_back, tab_ref[cols, :lanes])
        ).astype(low)

    pair = 2 * HEAD_DIM

    @pl.loop(0, width // pair)
    def _(p):
        cols = pl.ds(pl.multiple_of(p * pair, pair), pair)
        left = lax.broadcasted_iota(jnp.int32, (length, pair), 1) < HEAD_DIM
        query, key, value = q_ref[:, cols], k_ref[:, cols], v_ref[:, cols]
        given = cback_ref[:, cols]
        made = []
        for h in range(2):
            mine = left if h == 0 else jnp.logical_not(left)
            zero = jnp.zeros_like(query)
            same = mask_ref[...] > 0.5
            scores = nt(key, jnp.where(mine, query, zero))
            log_total = lse_ref[pl.ds(2 * p + h, 1), :]
            weights = jnp.exp(jnp.where(same, scores * scaling, far) - log_total)
            weights_back = nt(value, jnp.where(mine, given, zero))
            dots = jnp.sum(weights * weights_back, axis=0, keepdims=True)
            scores_back = jnp.where(same, weights * (weights_back - dots), 0.0).astype(low)
            made.append(
                (
                    tn(scores_back, key),
                    nn(scores_back, query),
                    nn(weights.astype(low), given),
                )
            )
        dq_ref[:, cols] = (jnp.where(left, made[0][0], made[1][0]) * scaling).astype(low)
        dk_ref[:, cols] = (jnp.where(left, made[0][1], made[1][1]) * scaling).astype(low)
        dv_ref[:, cols] = jnp.where(left, made[0][2], made[1][2]).astype(low)

    backs = (dq_ref, dk_ref, dv_ref)
    inner_back = jnp.zeros((length, lanes), low)
    for t in range(3):
        inner_back = inner_back + only(
            nn(backs[t][...], tab_ref[:, lanes:]).astype(low), t * rank, (t + 1) * rank
        )
    inner_out = only(inner_ref[...], 3 * rank, 4 * rank)
    for t in range(3):
        fetch(t).wait()
    half = 4 * rank

    @pl.loop(0, width // tile)
    def _(j):
        cols = pl.ds(pl.multiple_of(j * tile, tile), tile)
        total = one_ref[:, cols] + nt(inner_back, tab_ref[cols, :lanes])
        for t in range(3):
            total = total + nt(backs[t][...], w_ref[t, cols, :])
        out_ref[:, cols] = total
        gt_ref[:half, cols] = (tn(inner_back, x_ref[:, cols]) + tn(inner_out_back, context_ref[:, cols]))[:half]
        grow = tn(inner_out, low_ref[:, cols])
        for t in range(3):
            grow = grow + tn(only(inner_ref[...], t * rank, (t + 1) * rank), backs[t][:, cols])
        gt_ref[half:, cols] = grow[:half]

    grad_ref[...] = gt_ref[...].T.astype(low)


def on_device(
    tokens,
    cotangent,
    segments,
    adapter_id,
    input_weight,
    output_weight,
    norm_gain,
    norm_shift,
    attention_down,
    attention_up,
    expand_weight,
    reduce_weight,
    expand_down,
    expand_up,
    reduce_down,
    reduce_up,
):
    devices = lax.axis_size("fsdp")
    tables, adapters, part, rank = attention_down.shape
    width = part * devices
    part_inner = reduce_weight.shape[0]
    inner_width = part_inner * devices
    lanes = adapters * rank
    x = tokens[0]
    length = x.shape[0]
    vmem_limit = 58 * 1024 * 1024

    def call(kernel, name, outs, scratch, inputs, spaces):
        return pl.pallas_call(
            kernel,
            name=name,
            out_shape=tuple(jax.ShapeDtypeStruct(s, d) for s, d in outs),
            in_specs=[
                pl.BlockSpec(memory_space=pl.ANY if a else pltpu.VMEM) for a in spaces
            ],
            out_specs=tuple(pl.BlockSpec(memory_space=pltpu.VMEM) for _ in outs),
            scratch_shapes=scratch,
            compiler_params=pltpu.CompilerParams(vmem_limit_bytes=vmem_limit),
        )(*inputs)

    packed_attention = jnp.concatenate(
        [
            input_weight.transpose(1, 0, 2).reshape(part, 3 * width),
            output_weight,
            attention_down.transpose(2, 0, 1, 3).reshape(part, tables * lanes),
            attention_up.transpose(3, 0, 1, 2).reshape(part, tables * lanes),
            jnp.pad(
                jnp.concatenate([norm_gain, norm_shift], axis=0).T, ((0, 0), (0, lanes - 4))
            ),
        ],
        axis=1,
    )
    packed_expand = jnp.concatenate(
        [
            expand_weight,
            expand_down.transpose(1, 0, 2).reshape(part, lanes),
            reduce_up.transpose(2, 0, 1).reshape(part, lanes),
        ],
        axis=1,
    )
    packed_reduce = jnp.concatenate(
        [
            reduce_weight,
            reduce_down.transpose(1, 0, 2).reshape(part_inner, lanes),
            expand_up.transpose(2, 0, 1).reshape(part_inner, lanes),
        ],
        axis=1,
    )
    whole = lax.all_gather(packed_attention, "fsdp", axis=0, tiled=True)
    whole_expand = lax.all_gather(packed_expand, "fsdp", axis=0, tiled=True)
    whole_reduce = lax.all_gather(packed_reduce, "fsdp", axis=0, tiled=True)

    def selection(slots):
        row = lax.broadcasted_iota(jnp.int32, (len(slots) * lanes, lanes), 0)
        col = lax.broadcasted_iota(jnp.int32, (len(slots) * lanes, lanes), 1)
        slot = jnp.zeros_like(row)
        for t, s in enumerate(slots):
            slot = jnp.where(row // lanes == t, s, slot)
        return (
            ((row % lanes) // rank == adapter_id[0])
            & (row % rank == col % rank)
            & (col // rank == slot)
        ).astype(low)

    off = 4 * width + 2 * tables * lanes
    norms = whole[:, off : off + 4].astype(wide).T
    seg_row = segments
    seg_col = segments.reshape(length, 1)

    dense = (length, width)
    q, k, v, context, lse, inner, tab, hidden = call(
        lambda *refs: attend_kernel(rank, *refs),
        "attend",
        [
            (dense, low),
            (dense, low),
            (dense, low),
            (dense, low),
            ((lanes, length), wide),
            ((length, lanes), low),
            ((width, 2 * lanes), low),
            (dense, wide),
        ],
        [
            pltpu.VMEM((4, width, width), low),
            pltpu.VMEM((width, 2 * tables * lanes), low),
            pltpu.VMEM((length, length), wide),
            pltpu.VMEM((length, lanes), wide),
            pltpu.SemaphoreType.DMA((5,)),
        ],
        (x, seg_row, seg_col, selection(range(tables)), whole),
        (0, 0, 0, 0, 1),
    )
    chunk = min(512, inner_width)
    chunks = inner_width // chunk
    output, one_back, grad_w, grad_f = call(
        lambda *refs: feed_kernel(rank, *refs),
        "feed",
        [
            (dense, low),
            (dense, wide),
            ((width, lanes), low),
            ((2 * rank, inner_width), low),
        ],
        [
            pltpu.VMEM((chunks, width, chunk), low),
            pltpu.VMEM((chunks, chunk, width), low),
            pltpu.VMEM((width, 2 * lanes), low),
            pltpu.VMEM((chunks, chunk, 2 * lanes), low),
            pltpu.VMEM((width, lanes), low),
            pltpu.VMEM((chunks, chunk, lanes), low),
            pltpu.VMEM(dense, low),
            pltpu.VMEM((chunks, length, chunk), low),
            pltpu.VMEM((chunks, length, chunk), wide),
            pltpu.VMEM(dense, wide),
            pltpu.VMEM(dense, low),
            pltpu.SemaphoreType.DMA((chunks + 1,)),
            pltpu.SemaphoreType.DMA((chunks,)),
            pltpu.SemaphoreType.DMA((chunks,)),
        ],
        (
            hidden,
            cotangent[0],
            norms,
            selection((0, 1)),
            selection((1, 0)),
            whole_expand,
            whole_reduce,
        ),
        (0, 0, 0, 0, 0, 1, 1),
    )
    tokens_back, grad_att = call(
        lambda *refs: attend_back_kernel(rank, *refs),
        "attend_back",
        [(dense, wide), ((width, lanes), low)],
        [
            pltpu.VMEM((4, width, width), low),
            pltpu.VMEM((length, length), wide),
            pltpu.VMEM(dense, low),
            pltpu.VMEM(dense, low),
            pltpu.VMEM(dense, low),
            pltpu.VMEM(dense, low),
            pltpu.VMEM(dense, low),
            pltpu.VMEM((2 * tables * rank, width), wide),
            pltpu.SemaphoreType.DMA((4,)),
        ],
        (x, seg_row, seg_col, q, k, v, context, lse, inner, tab, one_back, whole),
        (0, 0, 0, 0, 0, 0, 0, 0, 0, 0, 0, 1),
    )

    half = tables * rank
    per_feed = grad_w.reshape(devices, part, lanes)
    folded = 2 * rank * part_inner // lanes
    per_inner = (
        grad_f.reshape(2 * rank, devices, part_inner)
        .transpose(1, 0, 2)
        .reshape(devices, folded, lanes)
    )
    chosen = (jnp.arange(lanes, dtype=jnp.int32) == adapter_id[0]).astype(low)
    sent = jnp.concatenate(
        [
            per_feed,
            per_inner,
            jnp.broadcast_to(chosen, (devices, 8, lanes)),
        ],
        axis=1,
    )
    got_feed = lax.all_to_all(sent, "fsdp", 0, 0, tiled=True)
    got_att = lax.all_to_all(grad_att.reshape(devices, part, lanes), "fsdp", 0, 0, tiled=True)
    who = got_feed[:, -1, :adapters]

    def summed(got):
        return jnp.einsum("sa,sxc->axc", who, got, preferred_element_type=wide)

    total_feed = summed(got_feed[:, :-8])
    total = summed(got_att)
    down_grad = total[:, :, :half].reshape(adapters, part, tables, rank).transpose(2, 0, 1, 3)
    up_grad = total[:, :, half:].reshape(adapters, part, tables, rank).transpose(2, 0, 3, 1)
    expand_down_grad = total_feed[:, :part, :rank]
    reduce_up_grad = total_feed[:, :part, rank : 2 * rank].transpose(0, 2, 1)
    inner_total = total_feed[:, part:].reshape(adapters, 2 * rank, part_inner)
    expand_up_grad = inner_total[:, :rank]
    reduce_down_grad = inner_total[:, rank:].transpose(0, 2, 1)
    return (
        output[None],
        tokens_back[None],
        down_grad,
        up_grad,
        expand_down_grad,
        expand_up_grad,
        reduce_down_grad,
        reduce_up_grad,
    )


def solution(mesh):
    placed = (
        P("fsdp", None, None),
        P("fsdp", None, None),
        P("fsdp", None),
        P("fsdp"),
        P(None, "fsdp", None),
        P("fsdp", None),
        P(None, "fsdp"),
        P(None, "fsdp"),
        P(None, None, "fsdp", None),
        P(None, None, None, "fsdp"),
        P("fsdp", None),
        P("fsdp", None),
        P(None, "fsdp", None),
        P(None, None, "fsdp"),
        P(None, "fsdp", None),
        P(None, None, "fsdp"),
    )
    return jax.shard_map(
        on_device,
        mesh=mesh,
        in_specs=placed,
        out_specs=(
            P("fsdp", None, None),
            P("fsdp", None, None),
            P(None, None, "fsdp", None),
            P(None, None, None, "fsdp"),
            P(None, "fsdp", None),
            P(None, None, "fsdp"),
            P(None, "fsdp", None),
            P(None, None, "fsdp"),
        ),
        check_vma=False,
    )
```

time: 537 us -> 378 us (0.70); the launches traced: 530 us -> 377 us
  matrix products: 184 us -> 0.58 us
  Pallas kernels: 0 us -> 106 us
  other arithmetic: 40.2 us -> 9.11 us
  waiting for transfers between devices: 250 us -> 224 us
  local copies, waits for them, and re-layouts: 36.2 us -> 14.1 us
  starting transfers between devices: 3.46 us -> 9.08 us
    dot_general x61 -> x2, matrix products: 184 us -> 0.58 us  [summed(): return jnp.einsum('sa,sxc->axc', who, got, preferred_element_type=wide)]
    pallas_call x0 -> x3, Pallas kernels: none -> 106 us  [call(): pl.pallas_call(kernel, name=name, out_shape=tuple((jax.ShapeDtypeStruct(s...]
    all_gather x1, waiting for transfers between devices: 70.8 us -> 48 us  [on_device(): whole_expand = lax.all_gather(packed_expand, 'fsdp', axis=0, tiled=True)]
    reduce_sum x5 -> x0, other arithmetic: 13.3 us -> none  [the longest x1 9.78 us: attend_forward(): jnp.sum(jnp.exp(masked - largest), axis=-1, keepdims=True)]
    convert_element_type x5 -> x3, other arithmetic: 13.6 us -> 3.11 us  [the longest x2 3.11 us: selection(): return ((row % lanes // rank == adapter_id[0]) & (row % rank == col % ran...]
    reshape x5 -> x1, local copies, waits for them, and re-layouts: 7.44 us -> 0.86 us  [on_device(): seg_col = segments.reshape(length, 1)]
    another operation x4 -> x0, other arithmetic: 6.31 us -> none
    all_to_all x1 -> x2, starting transfers between devices: 3.34 us -> 8.96 us  [the longest x1 5.84 us: on_device(): lax.all_to_all(grad_att.reshape(devices, part, lanes), 'fsdp', 0, 0, tile...]
  transfers between devices with their start and end apart: 4 -> 5, of which waited for: 4 -> 4; matrix products, arithmetic and copies ran while one was open for 5% -> 4% of each run, Pallas kernels for 0% -> 17%
where the time goes in v2:
time: 378 us; the launch traced here: 377 us
  waiting for transfers between devices  224 us (59%)
  Pallas kernels  106 us (28%)
  between operations  14.7 us (4%)
  local copies, waits for them, and re-layouts  14.1 us (4%)
  other arithmetic  9.11 us (2%)
  starting transfers between devices  9.08 us (2%)
    pallas_call x3, Pallas kernels, call(): pl.pallas_call(kernel, name=name, out_shape=tuple((jax.ShapeDtypeStruct(s...  106 us
    all_gather x1, waiting for transfers between devices, on_device(): whole_reduce = lax.all_gather(packed_reduce, 'fsdp', axis=0, tiled=True)  87.7 us
    all_gather x1, waiting for transfers between devices, on_device(): whole = lax.all_gather(packed_attention, 'fsdp', axis=0, tiled=True)  81 us
    all_gather x1, waiting for transfers between devices, on_device(): whole_expand = lax.all_gather(packed_expand, 'fsdp', axis=0, tiled=True)  48 us
  transfers between devices with their start and end apart: 5, of which 4 were waited for; matrix products, arithmetic and copies ran while one was open for 4% of the time, Pallas kernels for 17%

profile of v2, /device:TPU:0, one launch (start us, length us, event | category | flops | bytes accessed | tf_op | source)
XLA Modules:
  0.0 377.4 jit_solution(1968927823229573060)
XLA Ops:
  7.2 0.0 copy-start.2
  7.2 0.0 copy-start.3
  7.2 0.0 copy-start.1
  7.2 0.0 copy-start.4
  7.2 0.0 all-gather.4.cloned.1.call-start
  7.3 1.0 copy.94
  8.3 1.0 copy.70
  9.2 1.0 copy.71
  10.2 0.7 pad_maximum_fusion.3
  10.9 0.1 copy.69
  11.0 0.8 constant_dynamic-update-slice_fusion.3
  11.9 0.0 copy-start
  11.9 0.7 copy-done
  12.6 0.0 all-gather.4.cloned.1.call-update
  12.7 0.0 all-gather.6.cloned.1.call-start
  12.7 0.8 copy.73
  13.5 0.8 copy.74
  14.4 1.7 pad_maximum_fusion.2
  16.1 0.0 all-gather.6.cloned.1.call-update
  16.1 0.0 all-gather.8.cloned.1.call-start
  16.1 0.0 copy-done.2
  16.1 0.1 copy.75
  16.3 0.0 copy-done.3
  16.3 0.1 copy.76
  16.4 0.0 copy-done.1
  16.4 0.8 pad_maximum_fusion.1
  17.2 0.0 all-gather.8.cloned.1.call-update
  17.8 0.0 copy-done.4
  17.8 0.9 copy.72.refs_2_
  18.9 1.2 fusion.25
  20.1 1.9 fusion.12.refs_3_
  22.0 81.0 %all-gather.4.cloned.1.call-done.refs_4_.refs_11_ = bf16[1024,5248]{1,0:T(8,128)(2,1)} async-done(((bf16[32,5248]{1,0:T(8,128)(2,1)}), bf16[1024,5248]{1,0:T(8,128)(2,1)}) %all-gather.4.cloned.1.call-update) | async-done | bytes 10747920 | tf_op jit(solution)/shard_map/all_gather | solution.py:447
  103.0 1.0 convert_bitcast_fusion
  104.0 0.8 copy.77.refs_2_
  104.8 30.8 %attend.1 = (bf16[512,1024]{1,0:T(8,128)(2,1)}, bf16[512,1024]{1,0:T(8,128)(2,1)}, bf16[512,1024]{1,0:T(8,128)(2,1)}, bf16[512,1024]{1,0:T(8,128)(2,1)}, f32[128...) custom-call(bf16[512,1024]{1,0:T(8,128)(2,1)} %bitcast.58, ...), custom_call_target="tpu_custom_call" | custom-call | tf_op jit(solution)/shard_map/attend/pallas_call | solution.py:407
  135.6 48.0 %all-gather.6.cloned.1.call-done.refs_5_ = bf16[1024,4352]{1,0:T(8,128)(2,1)} async-done(((bf16[32,4352]{1,0:T(8,128)(2,1)}), bf16[1024,4352]{1,0:T(8,128)(2,1)}) %all-gather.6.cloned.1.call-update) | async-done | bytes 8912912 | tf_op jit(solution)/shard_map/all_gather | solution.py:448
  183.6 87.7 %all-gather.8.cloned.1.call-done.refs_6_ = bf16[4096,1280]{1,0:T(8,128)(2,1)} async-done(((bf16[128,1280]{1,0:T(8,128)(2,1)}), bf16[4096,1280]{1,0:T(8,128)(2,1)}) %all-gather.8.cloned.1.call-update) | async-done | bytes 10485776 | tf_op jit(solution)/shard_map/all_gather | solution.py:449
  271.2 41.3 %feed.1 = (bf16[512,1024]{1,0:T(8,128)(2,1)}, f32[512,1024]{1,0:T(8,128)}, bf16[1024,128]{1,0:T(8,128)(2,1)}, bf16[32,4096]{1,0:T(8,128)(2,1)}) custom-call(f32[512,1024]{1,0:T(8,128)} %get-tuple-element.22.refs_0_, bf16[512,1024]{1,0:T(8,128)(2,1)} %bitcast.60, f32[4,1024]{1,0:T(4,128)} %copy.77.refs_2_, bf16[256,128]{1,0:T(8,128)(2,1)} %get-tuple-element.67.refs_3_, ...), custom_call_target="tpu_custom_call" | custom-call | tf_op jit(solution)/shard_map/feed/pallas_call | solution.py:407
  312.5 1.0 bitcast_bitcast_fusion
  313.5 1.8 pad_maximum_fusion
  315.3 3.1 all-to-all-start
  318.4 34.0 %attend_back.1 = (f32[512,1024]{1,0:T(8,128)}, bf16[1024,128]{1,0:T(8,128)(2,1)}) custom-call(bf16[512,1024]{1,0:T(8,128)(2,1)} %bitcast.59, s32[1,512]{1,0:T(1,128)} %refs_1_.3, s32[512,1]{1,0:T(8,128)} %copy.72.refs_2_, bf16[512,1024]{1,0:T(8,128)(2,1)} %get-tuple-element.24.refs_3_, bf16[512,1024]{1,0:T(8,128)(2,1)} %get-tuple-element.25.refs_4_, ...), custom_call_target="tpu_custom_call" | custom-call | tf_op jit(solution)/shard_map/attend_back/pallas_call | solution.py:407
  352.4 0.0 all-to-all-done
  352.4 5.8 %all-to-all-start.1 = ((bf16[32,32,128]{2,1,0:T(8,128)(2,1)}), bf16[32,32,128]{2,1,0:T(8,128)(2,1)S(1)}, u32[]{:S(2)}, u32[]{:S(2)}) async-start(bf16[32,32,128]{2,1,0:T(8,128)(2,1)} %bitcast.64), calls=%async_computation.1 | async-start | bytes 524288 | tf_op jit(solution)/shard_map/all_to_all | solution.py:567
  358.3 0.1 copy.91
  358.4 0.1 slice.43
  358.5 0.4 fusion
  358.8 0.1 slice_bitcast_fusion
  358.9 0.7 copy.87
  359.7 0.7 copy.90
  360.4 0.6 copy.88
  361.1 0.6 copy.89
  361.7 7.1 %all-to-all-done.1 = bf16[32,32,128]{2,1,0:T(8,128)(2,1)S(1)} async-done(((bf16[32,32,128]{2,1,0:T(8,128)(2,1)}), bf16[32,32,128]{2,1,0:T(8,128)(2,1)S(1)}, u32[]{:S(2)}, u32[]{:S(2)}) %all-to-all-start.1) | async-done | bytes 262176 | tf_op jit(solution)/shard_map/all_to_all | solution.py:567
  368.9 0.2 fusion.7
  369.0 0.1 fusion.41
  369.1 0.1 copy.82
  369.3 0.7 copy.85
  370.0 0.1 copy.83
  370.2 0.7 copy.86
  (21 shorter events, 0.1 us)
Async XLA Ops:
  7.2 9.0 %copy-start.2 = (bf16[8,128,16]{1,2,0:T(8,128)(2,1)S(1)}, bf16[8,128,16]{1,2,0:T(8,128)(2,1)}, u32[]{:S(2)}) copy-start(bf16[8,128,16]{1,2,0:T(8,128)(2,1)} %param.30) | copy-start | bytes 98308
  7.2 9.1 %copy-start.3 = (bf16[8,16,128]{2,1,0:T(8,128)(2,1)S(1)}, bf16[8,16,128]{2,1,0:T(8,128)(2,1)}, u32[]{:S(2)}) copy-start(bf16[8,16,128]{2,1,0:T(8,128)(2,1)} %param.29) | copy-start | bytes 98308
  7.2 9.2 %copy-start.1 = (bf16[128,1024]{1,0:T(8,128)(2,1)S(1)}, bf16[128,1024]{1,0:T(8,128)(2,1)}, u32[]{:S(2)}) copy-start(bf16[128,1024]{1,0:T(8,128)(2,1)} %param.27) | copy-start | bytes 786436
  7.2 10.6 %copy-start.4 = (s32[1,512]{1,0:T(1,128)S(1)}, s32[1,512]{1,0:T(1,128)}, u32[]{:S(2)}) copy-start(s32[1,512]{1,0:T(1,128)} %refs_1_.3) | copy-start | bytes 6148
  7.2 95.8 %all-gather.4.cloned.1.call-start = ((), (), s32[]{:S(2)}) async-start(), calls=%async_computation.2 | async-start | bytes 11083776 | tf_op jit(solution)/shard_map/all_gather | solution.py:447
  11.9 0.7 copy-start
  12.7 170.9 %all-gather.6.cloned.1.call-start = ((), (), s32[]{:S(2)}) async-start(), calls=%async_computation.3 | async-start | bytes 9191424 | tf_op jit(solution)/shard_map/all_gather | solution.py:448
  16.1 255.1 %all-gather.8.cloned.1.call-start = ((), (), s32[]{:S(2)}) async-start(), calls=%async_computation.4 | async-start | bytes 10813440 | tf_op jit(solution)/shard_map/all_gather | solution.py:449
  315.3 37.1 %all-to-all-start = ((bf16[32,72,128]{2,1,0:T(8,128)(2,1)}), bf16[32,72,128]{2,1,0:T(8,128)(2,1)S(1)}, u32[]{:S(2)}, u32[]{:S(2)}) async-start(bf16[32,72,128]{2,1,0:T(8,128)(2,1)} %pad_maximum_fusion), calls=%async_computation | async-start | bytes 1179648 | tf_op jit(solution)/shard_map/all_to_all | solution.py:566
  352.4 16.4 %all-to-all-start.1 = ((bf16[32,32,128]{2,1,0:T(8,128)(2,1)}), bf16[32,32,128]{2,1,0:T(8,128)(2,1)S(1)}, u32[]{:S(2)}, u32[]{:S(2)}) async-start(bf16[32,32,128]{2,1,0:T(8,128)(2,1)} %bitcast.64), calls=%async_computation.1 | async-start | bytes 524288 | tf_op jit(solution)/shard_map/all_to_all | solution.py:567
Sparse Core Ops, SparseCore 0:
  12.8 90.1 all-gather.3
  105.8 77.6 all-gather.5
  186.4 84.7 all-gather.7
